TPU v7x, 32 devices: a whole 2x2x4 slice. The times are simulated.
32 devices in a mesh: fsdp: 8 (over z, y), seq: 4 (over x, core).
Axes of the slice: x: 2, y: 2, z: 4, core: 2. Of those that a mesh axis runs over, the one named last changes fastest.
Arguments:
- tokens: bfloat16 [16, 1024, 1024], P('fsdp', 'seq'), may hold values from -6 to 6
- first_gain: float32 [1024], replicated, may hold values from 0.5 to 1.5
- first_shift: float32 [1024], replicated, may hold values from -1 to 1
- attention_weight: bfloat16 [1024, 3072], P('fsdp', 'seq'), may hold values from -0.25 to 0.25
- attention_bias: float32 [3072], replicated, may hold values from -1.5 to 1.5
- output_weight: bfloat16 [1024, 1024], P('fsdp', 'seq'), may hold values from -1.5 to 1.5
- output_bias: float32 [1024], replicated, may hold values from -1 to 1
- second_gain: float32 [1024], replicated, may hold values from 0.5 to 1.5
- second_shift: float32 [1024], replicated, may hold values from -1 to 1
- expand_weight: bfloat16 [1024, 4096], P('fsdp', 'seq'), may hold values from -0.1875 to 0.1875
- expand_bias: float32 [4096], replicated, may hold values from -1 to 1
- contract_weight: bfloat16 [4096, 1024], P('fsdp', 'seq'), may hold values from -0.1875 to 0.1875
- contract_bias: float32 [1024], replicated, may hold values from -1 to 1
- cotangent: bfloat16 [16, 1024, 1024], P('fsdp', 'seq'), may hold values from -6 to 6
- threshold: float32 [1], replicated, may hold values from 3 to 6
Outputs:
- block_output: bfloat16 [16, 1024, 1024], P('fsdp', 'seq')
- input_grad: float32 [16, 1024, 1024], P('fsdp', 'seq')
- grad_first_gain: float32 [1024], replicated
- grad_first_shift: float32 [1024], replicated
- grad_attention_weight: float32 [1024, 3072], P('fsdp', 'seq')
- grad_attention_bias: float32 [3072], replicated
- grad_output_weight: float32 [1024, 1024], P('fsdp', 'seq')
- grad_output_bias: float32 [1024], replicated
- grad_second_gain: float32 [1024], replicated
- grad_second_shift: float32 [1024], replicated
- grad_expand_weight: float32 [1024, 4096], P('fsdp', 'seq')
- grad_expand_bias: float32 [4096], replicated
- grad_contract_weight: float32 [4096, 1024], P('fsdp', 'seq')
- grad_contract_bias: float32 [1024], replicated
- head_peak: float32 [16], P('seq')
- clipped_weight: float32 [1024, 3072], P('fsdp', 'seq')
- clipped_bias: float32 [3072], P('seq')
All inputs are finite; a program needn't handle non-finite values.
Results may differ from a plain program's by a relative error of at most 0.018.
Values may be sent and summed in bfloat16 or wider, within the bound.
No kernel may reach another device: no remote copies, remote signals or barrier semaphores. Data moves between devices by JAX's collectives and lax.ppermute only.
A program may use at most 320 MiB of HBM per device.

v0:
```python
import jax
import jax.numpy as jnp
from jax import lax
from jax.sharding import PartitionSpec as P

D = 1024
H = 16
HD = 64
QBLK = 512


def layer_norm(values, gain, shift):
    centered = values - jnp.mean(values, axis=-1, keepdims=True)
    variance = jnp.mean(centered * centered, axis=-1, keepdims=True)
    return centered * lax.rsqrt(variance + 1e-05) * gain + shift


def gelu_tanh(values):
    return jax.nn.gelu(values, approximate=True)


def causal_mask(row_start, row_stop):
    row_ids = row_start + jnp.arange(row_stop - row_start)[:, None]
    col_ids = jnp.arange(row_stop)[None, :]
    return col_ids <= row_ids


def block_logits(query_block, keys_part, row_start, row_stop, logit_scale):
    logits = (
        jnp.einsum("nqhd,nkhd->nhqk", query_block, keys_part, preferred_element_type=jnp.float32)
        * logit_scale
    )
    return jnp.where(causal_mask(row_start, row_stop), logits, -jnp.inf)


def split_packed(packed):
    head_size = packed.shape[-1] // 3
    return (
        packed[..., :head_size],
        packed[..., head_size : 2 * head_size],
        packed[..., 2 * head_size :],
    )


def attend_forward(packed):
    queries, keys_all, values_all = split_packed(packed)
    length = packed.shape[1]
    logit_scale = queries.shape[-1] ** (-0.5)
    outputs = []
    log_sums = []
    peak_value = None
    for block_index in range(length // QBLK):
        row_start = block_index * QBLK
        row_stop = row_start + QBLK
        logits = block_logits(
            queries[:, row_start:row_stop], keys_all[:, :row_stop], row_start, row_stop, logit_scale
        )
        row_top = jnp.max(logits, axis=-1, keepdims=True)
        shifted = jnp.exp(logits - row_top)
        row_total = jnp.sum(shifted, axis=-1, keepdims=True)
        probabilities = (shifted / row_total).astype(jnp.bfloat16)
        block_out = jnp.einsum(
            "nhqk,nkhd->nqhd",
            probabilities,
            values_all[:, :row_stop],
            preferred_element_type=jnp.float32,
        )
        outputs.append(block_out.astype(jnp.bfloat16))
        log_sums.append((row_top + jnp.log(row_total))[..., 0])
        block_peak = jnp.max(row_top[..., 0], axis=-1)
        peak_value = block_peak if peak_value is None else jnp.maximum(peak_value, block_peak)
    return (jnp.concatenate(outputs, axis=1), jnp.concatenate(log_sums, axis=-1), peak_value)


def attend_items(packed):
    attended, log_sums, peak_value = attend_forward(packed)
    returned = lax.all_to_all(attended, "seq", split_axis=1, concat_axis=2, tiled=True)
    return (returned, log_sums, peak_value, packed)


def attend_backward(packed, log_sums, heads_cot):
    queries, keys_all, values_all = split_packed(packed)
    length = packed.shape[1]
    logit_scale = queries.shape[-1] ** (-0.5)
    query_grads = []
    key_grad = jnp.zeros(keys_all.shape, jnp.float32)
    value_grad = jnp.zeros(values_all.shape, jnp.float32)
    for block_index in range(length // QBLK):
        row_start = block_index * QBLK
        row_stop = row_start + QBLK
        query_block = queries[:, row_start:row_stop]
        cot_block = heads_cot[:, row_start:row_stop]
        logits = block_logits(query_block, keys_all[:, :row_stop], row_start, row_stop, logit_scale)
        probabilities = jnp.exp(logits - log_sums[:, :, row_start:row_stop, None])
        prob_grad = jnp.einsum(
            "nqhd,nkhd->nhqk",
            cot_block,
            values_all[:, :row_stop],
            preferred_element_type=jnp.float32,
        )
        row_inner = jnp.sum(prob_grad * probabilities, axis=-1, keepdims=True)
        logit_grad = (probabilities * (prob_grad - row_inner)).astype(jnp.bfloat16)
        query_grads.append(
            jnp.einsum(
                "nhqk,nkhd->nqhd",
                logit_grad,
                keys_all[:, :row_stop],
                preferred_element_type=jnp.float32,
            )
            * logit_scale
        )
        key_grad = key_grad.at[:, :row_stop].add(
            jnp.einsum(
                "nhqk,nqhd->nkhd", logit_grad, query_block, preferred_element_type=jnp.float32
            )
            * logit_scale
        )
        value_grad = value_grad.at[:, :row_stop].add(
            jnp.einsum(
                "nhqk,nqhd->nkhd",
                probabilities.astype(jnp.bfloat16),
                cot_block,
                preferred_element_type=jnp.float32,
            )
        )
    joined = jnp.concatenate([jnp.concatenate(query_grads, axis=1), key_grad, value_grad], axis=-1)
    return joined.astype(jnp.bfloat16)


def body(
    tokens,
    first_gain,
    first_shift,
    attention_weight,
    attention_bias,
    output_weight,
    output_bias,
    second_gain,
    second_shift,
    expand_weight,
    expand_bias,
    contract_weight,
    contract_bias,
    cotangent,
    threshold,
):
    partial_full = (
        lax.all_gather(attention_weight, "seq", axis=1, tiled=True),
        lax.all_gather(output_weight, "seq", axis=1, tiled=True),
        lax.all_gather(expand_weight, "seq", axis=1, tiled=True),
        lax.all_gather(contract_weight, "seq", axis=1, tiled=True),
    )
    full_weights = (
        lax.all_gather(partial_full[0], "fsdp", axis=0, tiled=True),
        lax.all_gather(partial_full[1], "fsdp", axis=0, tiled=True),
        lax.all_gather(partial_full[2], "fsdp", axis=0, tiled=True),
        lax.all_gather(partial_full[3], "fsdp", axis=0, tiled=True),
    )
    mixing_full, output_full, expand_full, contract_full = full_weights
    seq_here = tokens.shape[0]
    tok_here = tokens.shape[1]
    tokens_float = tokens.astype(jnp.float32)
    normed_first = layer_norm(tokens_float, first_gain, first_shift).astype(jnp.bfloat16)
    mixed = (
        jnp.einsum("ntd,de->nte", normed_first, mixing_full, preferred_element_type=jnp.float32)
        + attention_bias
    )
    mixed = mixed.astype(jnp.bfloat16).reshape(seq_here, tok_here, H, 3 * HD)
    returned, log_sums, peaks, packed = attend_items(
        lax.all_to_all(mixed, "seq", split_axis=2, concat_axis=1, tiled=True)
    )
    attended = returned.reshape(seq_here, tok_here, D)
    residual = (
        tokens_float
        + jnp.einsum("nte,ed->ntd", attended, output_full, preferred_element_type=jnp.float32)
        + output_bias
    )
    normed_second = layer_norm(residual, second_gain, second_shift).astype(jnp.bfloat16)
    hidden = (
        jnp.einsum("ntd,di->nti", normed_second, expand_full, preferred_element_type=jnp.float32)
        + expand_bias
    )
    active = gelu_tanh(hidden).astype(jnp.bfloat16)
    result = (
        residual
        + jnp.einsum("nti,id->ntd", active, contract_full, preferred_element_type=jnp.float32)
        + contract_bias
    )
    block_output = result.astype(jnp.bfloat16)
    cot_float = cotangent.astype(jnp.float32)
    grad_contract = jnp.einsum("nti,ntd->id", active, cotangent, preferred_element_type=jnp.float32)
    grad_contract_bias = jnp.sum(cot_float, axis=(0, 1))
    active_cot = jnp.einsum(
        "ntd,id->nti", cotangent, contract_full, preferred_element_type=jnp.float32
    )
    _, gelu_pull = jax.vjp(gelu_tanh, hidden)
    hidden_cot = gelu_pull(active_cot)[0].astype(jnp.bfloat16)
    grad_expand = jnp.einsum(
        "ntd,nti->di", normed_second, hidden_cot, preferred_element_type=jnp.float32
    )
    grad_expand_bias = jnp.sum(hidden_cot.astype(jnp.float32), axis=(0, 1))
    second_cot = jnp.einsum(
        "nti,di->ntd", hidden_cot, expand_full, preferred_element_type=jnp.float32
    )
    _, second_pull = jax.vjp(layer_norm, residual, second_gain, second_shift)
    residual_part, grad_second_gain, grad_second_shift = second_pull(second_cot)
    residual_cot = cot_float + residual_part
    branch_cot = residual_cot.astype(jnp.bfloat16)
    grad_output = jnp.einsum(
        "nte,ntd->ed", attended, branch_cot, preferred_element_type=jnp.float32
    )
    grad_output_bias = jnp.sum(branch_cot.astype(jnp.float32), axis=(0, 1))
    attended_cot = jnp.einsum(
        "ntd,ed->nte", branch_cot, output_full, preferred_element_type=jnp.float32
    )
    attended_cot = attended_cot.astype(jnp.bfloat16).reshape(seq_here, tok_here, H, HD)
    heads_cot = lax.all_to_all(attended_cot, "seq", split_axis=2, concat_axis=1, tiled=True)
    packed_cot = attend_backward(packed, log_sums, heads_cot)
    mixed_cot = lax.all_to_all(packed_cot, "seq", split_axis=1, concat_axis=2, tiled=True).reshape(
        seq_here, tok_here, 3 * D
    )
    grad_mixing = jnp.einsum(
        "ntd,nte->de", normed_first, mixed_cot, preferred_element_type=jnp.float32
    )
    grad_mixing_bias = jnp.sum(mixed_cot.astype(jnp.float32), axis=(0, 1))
    first_cot = jnp.einsum(
        "nte,de->ntd", mixed_cot, mixing_full, preferred_element_type=jnp.float32
    )
    _, first_pull = jax.vjp(layer_norm, tokens_float, first_gain, first_shift)
    token_part, grad_first_gain, grad_first_shift = first_pull(first_cot)
    input_grad = residual_cot + token_part
    summed_first = (
        lax.psum_scatter(
            grad_mixing.astype(jnp.bfloat16), "fsdp", scatter_dimension=0, tiled=True
        ).astype(jnp.float32),
        lax.psum_scatter(
            grad_output.astype(jnp.bfloat16), "fsdp", scatter_dimension=0, tiled=True
        ).astype(jnp.float32),
        lax.psum_scatter(
            grad_expand.astype(jnp.bfloat16), "fsdp", scatter_dimension=0, tiled=True
        ).astype(jnp.float32),
        lax.psum_scatter(
            grad_contract.astype(jnp.bfloat16), "fsdp", scatter_dimension=0, tiled=True
        ).astype(jnp.float32),
    )
    weight_grads = (
        lax.psum_scatter(
            summed_first[0].astype(jnp.bfloat16), "seq", scatter_dimension=1, tiled=True
        ).astype(jnp.float32),
        lax.psum_scatter(
            summed_first[1].astype(jnp.bfloat16), "seq", scatter_dimension=1, tiled=True
        ).astype(jnp.float32),
        lax.psum_scatter(
            summed_first[2].astype(jnp.bfloat16), "seq", scatter_dimension=1, tiled=True
        ).astype(jnp.float32),
        lax.psum_scatter(
            summed_first[3].astype(jnp.bfloat16), "seq", scatter_dimension=1, tiled=True
        ).astype(jnp.float32),
    )
    vector_totals = lax.psum(
        (
            grad_first_gain,
            grad_first_shift,
            grad_mixing_bias,
            grad_output_bias,
            grad_second_gain,
            grad_second_shift,
            grad_expand_bias,
            grad_contract_bias,
        ),
        ("fsdp", "seq"),
    )
    head_peak = lax.pmax(jnp.max(peaks, axis=0), "fsdp")
    rows_here = attention_weight.shape[0]
    col_width = attention_weight.shape[1]
    heads_here = head_peak.shape[0]
    head_size = col_width // (3 * heads_here)
    factor = jnp.sqrt(threshold[0] / jnp.maximum(head_peak, threshold[0]))
    multiplier = jnp.stack([factor, factor, jnp.ones_like(factor)], axis=1)
    clipped_weight = (
        attention_weight.astype(jnp.float32).reshape(rows_here, heads_here, 3, head_size)
        * multiplier[None, :, :, None]
    ).reshape(rows_here, col_width)
    bias_piece = lax.dynamic_slice_in_dim(
        attention_bias, lax.axis_index("seq") * col_width, col_width
    )
    clipped_bias = (bias_piece.reshape(heads_here, 3, head_size) * multiplier[:, :, None]).reshape(
        col_width
    )
    return (
        block_output,
        input_grad,
        vector_totals[0],
        vector_totals[1],
        weight_grads[0],
        vector_totals[2],
        weight_grads[1],
        vector_totals[3],
        vector_totals[4],
        vector_totals[5],
        weight_grads[2],
        vector_totals[6],
        weight_grads[3],
        vector_totals[7],
        head_peak,
        clipped_weight,
        clipped_bias,
    )


def solution(mesh):
    placed = (
        P("fsdp", "seq", None),
        P(),
        P(),
        P("fsdp", "seq"),
        P(),
        P("fsdp", "seq"),
        P(),
        P(),
        P(),
        P("fsdp", "seq"),
        P(),
        P("fsdp", "seq"),
        P(),
        P("fsdp", "seq", None),
        P(),
    )
    return jax.shard_map(
        body,
        mesh=mesh,
        in_specs=placed,
        out_specs=(
            P("fsdp", "seq", None),
            P("fsdp", "seq", None),
            P(),
            P(),
            P("fsdp", "seq"),
            P(),
            P("fsdp", "seq"),
            P(),
            P(),
            P(),
            P("fsdp", "seq"),
            P(),
            P("fsdp", "seq"),
            P(),
            P("seq"),
            P("fsdp", "seq"),
            P("seq"),
        ),
        check_vma=False,
    )
```

profile of v0, /device:TPU:0, one launch (start us, length us, event | category | flops | bytes accessed | tf_op | source)
XLA Modules:
  0.0 1167.2 jit_solution(12801582693143362905)
XLA Ops:
  8.8 11.7 %all_gather.24 = bf16[128,3072]{1,0:T(8,128)(2,1)} all-gather(bf16[128,768]{1,0:T(8,128)(2,1)} %param.30), channel_id=1, replica_groups=mesh['fsdp'=8,'seq'=4] {'seq'}, dimensions={1}, use_global_device_ids=true | all-gather | bytes 983040 | tf_op jit(solution)/shard_map/all_gather | solution.py:148
  20.5 8.3 all_gather.26
  30.6 18.4 %all-gather.15.cloned.1.call-done = bf16[512,1024]{1,0:T(8,128)(2,1)} async-done(((bf16[512,256]{1,0:T(8,128)(2,1)}), bf16[512,1024]{1,0:T(8,128)(2,1)}) %all-gather.15.cloned.1.call-update) | async-done | bytes 1048592 | tf_op jit(solution)/shard_map/all_gather | solution.py:151
  49.6 100.5 %all-gather.7.cloned.1.call-done = bf16[1024,3072]{1,0:T(8,128)(2,1)} async-done(((bf16[128,3072]{1,0:T(8,128)(2,1)}), bf16[1024,3072]{1,0:T(8,128)(2,1)}) %all-gather.7.cloned.1.call-update) | async-done | bytes 6291472 | tf_op jit(solution)/shard_map/all_gather | solution.py:154
  150.2 7.8 add_convert_fusion
  172.2 36.5 %all-to-all-done = bf16[2,256,16,192]{1,3,0,2:T(8,128)(2,1)} async-done(((bf16[2,256,16,192]{1,3,0,2:T(8,128)(2,1)}), bf16[2,256,16,192]{1,3,0,2:T(8,128)(2,1)}, u32[]{:S(2)}, u32[]{:S(2)}) %all-to-all-start) | async-done | bytes 3145760 | tf_op jit(solution)/shard_map/all_to_all | solution.py:170
  208.7 6.3 copy.158
  248.0 18.9 %all_to_all.66 = bf16[4,2,65536]{2,1,0:T(2,128)(2,1)} all-to-all(bf16[4,2,65536]{2,1,0:T(2,128)(2,1)} %reshape.309), channel_id=1, replica_groups=mesh['fsdp'=8,'seq'=4] {'seq'}, dimensions={0} | all-to-all | bytes 2097152 | tf_op jit(solution)/shard_map/all_to_all | solution.py:77
  276.3 48.9 %all-gather.13.cloned.1.call-done = bf16[1024,4096]{1,0:T(8,128)(2,1)} async-done(((bf16[128,4096]{1,0:T(8,128)(2,1)}), bf16[1024,4096]{1,0:T(8,128)(2,1)}) %all-gather.13.cloned.1.call-update) | async-done | bytes 8388624 | tf_op jit(solution)/shard_map/all_gather | solution.py:156
  325.2 10.2 fusion.17
  335.4 114.9 %all-gather.17.cloned.1.call-done = bf16[4096,1024]{1,0:T(8,128)(2,1)} async-done(((bf16[512,1024]{1,0:T(8,128)(2,1)}), bf16[4096,1024]{1,0:T(8,128)(2,1)}) %all-gather.17.cloned.1.call-update) | async-done | bytes 8388624 | tf_op jit(solution)/shard_map/all_gather | solution.py:157
  450.4 14.6 %convert_reduce_fusion = (f32[4096]{0:T(1024)}, bf16[2,256,4096]{2,1,0:T(8,128)(2,1)S(1)}) fusion(f32[2,256,4096]{2,1,0:T(8,128)} %fusion.17, f32[4096]{0:T(1024)S(1)} %copy-done.41, bf16[2,256,1024]{2,1,0:T(8,128)(2,1)} %param.40, bf16[4096,1024]{1,0:T(8,128)(2,1)} %all-gather.17.cloned.1.call-done), kind=kOutput, calls=%fused_computation.29 | convolution fusion | flops 4343197696 | bytes 22052864 | tf_op jit(solution)/shard_map/ntd,id->nti/dot_general | solution.py:193
  486.9 9.9 all-to-all-done.2
  506.7 7.6 fusion.99
  526.2 10.9 fusion.98
  537.1 7.9 multiply_convert_fusion
  560.0 7.6 copy.170
  567.6 53.8 %all_to_all.67 = bf16[2,1024,4,192]{3,2,0,1:T(4,128)(2,1)} all-to-all(bf16[2,1024,4,192]{3,2,0,1:T(4,128)(2,1)} %copy.170), channel_id=1, replica_groups=mesh['fsdp'=8,'seq'=4] {'seq'}, dimensions={1} | all-to-all | bytes 6291456 | tf_op jit(solution)/shard_map/all_to_all | solution.py:219
  621.5 7.3 copy.172
  628.7 7.7 bitcast_convert_fusion.2
  637.7 13.1 %bitcast_convert_fusion = bf16[4096,1024]{1,0:T(8,128)(2,1)} fusion(bf16[2,256,1024]{2,1,0:T(8,128)(2,1)S(1)} %copy-done.12, f32[2,256,4096]{2,1,0:T(8,128)} %fusion.17, f32[4096]{0:T(1024)S(1)} %copy-done.42), kind=kOutput, calls=%fused_computation | convolution fusion | flops 4320133120 | bytes 17842176 | tf_op jit(solution)/shard_map/nti,ntd->id/dot_general | solution.py:191
  652.4 9.5 bitcast_convert_fusion.1
  662.7 89.2 %reduce-scatter.9.cloned.1.call-done = bf16[128,3072]{1,0:T(8,128)(2,1)} async-done(((bf16[1024,3072]{1,0:T(8,128)(2,1)}), bf16[128,3072]{1,0:T(8,128)(2,1)}) %reduce-scatter.9.cloned.1.call-update) | async-done | bytes 786448 | tf_op jit(solution)/shard_map/reduce_scatter | solution.py:233
  752.7 151.0 %reduce-scatter.21.cloned.1.call-done = bf16[512,1024]{1,0:T(8,128)(2,1)} async-done(((bf16[4096,1024]{1,0:T(8,128)(2,1)}), bf16[512,1024]{1,0:T(8,128)(2,1)}) %reduce-scatter.21.cloned.1.call-update) | async-done | bytes 1048592 | tf_op jit(solution)/shard_map/reduce_scatter | solution.py:242
  903.8 12.2 %add_convert_fusion.1 = bf16[2,256,1024]{2,1,0:T(8,128)(2,1)} fusion(f32[2,256,1024]{2,1,0:T(8,128)S(1)} %copy-done.6, bf16[4096,1024]{1,0:T(8,128)(2,1)} %all-gather.17.cloned.1.call-done, f32[1024]{0:T(1024)S(1)} %copy-done.47, f32[2,256,4096]{2,1,0:T(8,128)} %fusion.17, f32[4096]{0:T(1024)S(1)} %copy-done.42), kind=kOutput, calls=%fused_computation.83 | convolution fusion | flops 4317511680 | bytes 19943424 | tf_op jit(solution)/shard_map/nti,id->ntd/dot_general | solution.py:186
  916.0 20.6 %pmax.7 = f32[4]{0:T(128)S(1)} all-reduce(f32[4]{0:T(128)S(1)} %maximum_reduce_fusion), channel_id=1, replica_groups=mesh['fsdp'=8,'seq'=4] {'fsdp'}, use_global_device_ids=true, to_apply=%region_41.42 | all-reduce | flops 4 | bytes 32 | tf_op jit(solution)/shard_map/pmax | solution.py:273
  939.2 8.0 copy.193
  950.7 105.3 %reduce-scatter.17.cloned.1.call-done = bf16[128,4096]{1,0:T(8,128)(2,1)} async-done(((bf16[1024,4096]{1,0:T(8,128)(2,1)}), bf16[128,4096]{1,0:T(8,128)(2,1)}) %reduce-scatter.17.cloned.1.call-update) | async-done | bytes 1048592 | tf_op jit(solution)/shard_map/reduce_scatter | solution.py:239
  1056.0 7.0 fusion.100
  1066.7 40.8 %all-reduce.2 = (f32[1024]{0:T(1024)}, f32[1024]{0:T(1024)}, f32[3072]{0:T(1024)}, f32[1024]{0:T(1024)}, f32[1024]{0:T(1024)}, /*index=5*/f32[1024]{0:T(1024)}, f32[4096]{0:T(1024)}, f32[1024]{0:T(1024)}) all-reduce(f32[1024]{0:T(1024)S(1)} %get-tuple-element.87, ...), channel_id=1, replica_groups=mesh['fsdp'=8,'seq'=4] {'fsdp','seq'}, use_global_device_ids=true, to_apply=%region_15.16 | all-reduce | flops 13312 | bytes 106496 | tf_op jit(solution)/shard_map/psum | solution.py:260
  1110.7 20.5 %reduce-scatter.23.cloned.1.call-done = bf16[512,256]{1,0:T(8,128)(2,1)} async-done(((bf16[512,1024]{1,0:T(8,128)(2,1)}), bf16[512,256]{1,0:T(8,128)(2,1)}) %reduce-scatter.23.cloned.1.call-update) | async-done | bytes 262160 | tf_op jit(solution)/shard_map/reduce_scatter | solution.py:256
  1133.0 25.7 %reduce-scatter.19.cloned.1.call-done = bf16[128,1024]{1,0:T(8,128)(2,1)} async-done(((bf16[128,4096]{1,0:T(8,128)(2,1)}), bf16[128,1024]{1,0:T(8,128)(2,1)}) %reduce-scatter.19.cloned.1.call-update) | async-done | bytes 262160 | tf_op jit(solution)/shard_map/reduce_scatter | solution.py:253
  (215 shorter events, 139.3 us)
Async XLA Ops:
  7.2 41.8 %copy-start.2 = (bf16[2,256,1024]{2,1,0:T(8,128)(2,1)S(1)}, bf16[2,256,1024]{2,1,0:T(8,128)(2,1)}, u32[]{:S(2)}) copy-start(bf16[2,256,1024]{2,1,0:T(8,128)(2,1)} %param.27) | copy-start | bytes 3145732
  7.2 143.0 %copy-start.28 = (f32[1024]{0:T(1024)S(1)}, f32[1024]{0:T(1024)}, u32[]{:S(2)}) copy-start(f32[1024]{0:T(1024)} %param.28) | copy-start | bytes 12292
  7.2 143.0 %copy-start.39 = (f32[3072]{0:T(1024)S(1)}, f32[3072]{0:T(1024)}, u32[]{:S(2)}) copy-start(f32[3072]{0:T(1024)} %param.31) | copy-start | bytes 36868
  7.2 143.0 %copy-start.43 = (f32[1024]{0:T(1024)S(1)}, f32[1024]{0:T(1024)}, u32[]{:S(2)}) copy-start(f32[1024]{0:T(1024)} %param.29) | copy-start | bytes 12292
  7.2 23.3 %all-gather.11.cloned.1.call-start = ((), (), s32[]{:S(2)}) async-start(), calls=%async_computation.14 | async-start | bytes 1310720 | tf_op jit(solution)/shard_map/all_gather | solution.py:150
  8.0 41.0 %all-gather.15.cloned.1.call-start = ((), (), s32[]{:S(2)}) async-start(), calls=%async_computation.16 | async-start | bytes 1310720 | tf_op jit(solution)/shard_map/all_gather | solution.py:151
  8.7 141.5 %all-gather.7.cloned.1.call-start = ((), (), s32[]{:S(2)}) async-start(), calls=%async_computation.12 | async-start | bytes 7077888 | tf_op jit(solution)/shard_map/all_gather | solution.py:154
  20.5 252.2 %all-gather.9.cloned.1.call-start = ((), (), s32[]{:S(2)}) async-start(), calls=%async_computation.13 | async-start | bytes 2359296 | tf_op jit(solution)/shard_map/all_gather | solution.py:155
  28.9 296.4 %all-gather.13.cloned.1.call-start = ((), (), s32[]{:S(2)}) async-start(), calls=%async_computation.15 | async-start | bytes 9437184 | tf_op jit(solution)/shard_map/all_gather | solution.py:156
  30.5 419.8 %all-gather.17.cloned.1.call-start = ((), (), s32[]{:S(2)}) async-start(), calls=%async_computation.17 | async-start | bytes 9437184 | tf_op jit(solution)/shard_map/all_gather | solution.py:157
  49.2 108.8 %copy-start.21 = (f32[2,256]{1,0:T(2,128)}, f32[2,256]{1,0:T(2,128)S(1)}, u32[]{:S(2)}) copy-start(f32[2,256]{1,0:T(2,128)S(1)} %broadcast_multiply_fusion.1) | copy-start | bytes 6148
  49.6 108.4 %copy-start.25 = (f32[2,256]{1,0:T(2,128)}, f32[2,256]{1,0:T(2,128)S(1)}, u32[]{:S(2)}) copy-start(f32[2,256]{1,0:T(2,128)S(1)} %fusion.44) | copy-start | bytes 6148
  49.6 108.4 %copy-start.23 = (f32[2,256]{1,0:T(2,128)}, f32[2,256]{1,0:T(2,128)S(1)}, u32[]{:S(2)}) copy-start(f32[2,256]{1,0:T(2,128)S(1)} %fusion.96) | copy-start | bytes 6148
  166.7 42.0 %all-to-all-start = ((bf16[2,256,16,192]{1,3,0,2:T(8,128)(2,1)}), bf16[2,256,16,192]{1,3,0,2:T(8,128)(2,1)}, u32[]{:S(2)}, u32[]{:S(2)}) async-start(bf16[2,256,16,192]{1,3,0,2:T(8,128)(2,1)} %copy.156), calls=%async_computation | async-start | bytes 6291456 | tf_op jit(solution)/shard_map/all_to_all | solution.py:170
  272.6 52.6 %copy-start.37 = (f32[1024]{0:T(1024)S(1)}, f32[1024]{0:T(1024)}, u32[]{:S(2)}) copy-start(f32[1024]{0:T(1024)} %param.34) | copy-start | bytes 12292
  272.6 52.6 %copy-start.45 = (f32[1024]{0:T(1024)S(1)}, f32[1024]{0:T(1024)}, u32[]{:S(2)}) copy-start(f32[1024]{0:T(1024)} %param.35) | copy-start | bytes 12292
  275.9 194.5 %copy-start.5 = (f32[2,256,1024]{2,1,0:T(8,128)}, f32[2,256,1024]{2,1,0:T(8,128)S(1)}, u32[]{:S(2)}) copy-start(f32[2,256,1024]{2,1,0:T(8,128)S(1)} %get-tuple-element.111) | copy-start | bytes 6291460
  276.3 194.1 %copy-start.31 = (f32[2,256]{1,0:T(2,128)}, f32[2,256]{1,0:T(2,128)S(1)}, u32[]{:S(2)}) copy-start(f32[2,256]{1,0:T(2,128)S(1)} %fusion.97) | copy-start | bytes 6148
  276.3 174.0 %copy-start.41 = (f32[4096]{0:T(1024)S(1)}, f32[4096]{0:T(1024)}, u32[]{:S(2)}) copy-start(f32[4096]{0:T(1024)} %param.37) | copy-start | bytes 49156
  478.8 18.0 %all-to-all-start.2 = ((bf16[2,256,16,64]{1,3,0,2:T(8,128)(2,1)}), bf16[2,256,16,64]{1,3,0,2:T(8,128)(2,1)S(1)}, u32[]{:S(2)}, u32[]{:S(2)}) async-start(bf16[2,256,16,64]{1,3,0,2:T(8,128)(2,1)} %copy.165), calls=%async_computation.2 | async-start | bytes 2097152 | tf_op jit(solution)/shard_map/all_to_all | solution.py:217
  482.3 179.7 %reduce-scatter.13.cloned.1.call-start = ((), (), s32[]{:S(2)}) async-start(), calls=%async_computation.20 | async-start | bytes 2359296 | tf_op jit(solution)/shard_map/reduce_scatter | solution.py:236
  486.8 265.1 %reduce-scatter.9.cloned.1.call-start = ((), (), s32[]{:S(2)}) async-start(), calls=%async_computation.18 | async-start | bytes 7077888 | tf_op jit(solution)/shard_map/reduce_scatter | solution.py:233
  636.5 267.2 %reduce-scatter.21.cloned.1.call-start = ((), (), s32[]{:S(2)}) async-start(), calls=%async_computation.24 | async-start | bytes 9437184 | tf_op jit(solution)/shard_map/reduce_scatter | solution.py:242
  650.8 405.1 %reduce-scatter.17.cloned.1.call-start = ((), (), s32[]{:S(2)}) async-start(), calls=%async_computation.22 | async-start | bytes 9437184 | tf_op jit(solution)/shard_map/reduce_scatter | solution.py:239
  661.9 90.8 %copy-start.33 = (f32[2,4]{1,0:T(2,128)S(1)}, f32[2,4]{1,0:T(2,128)}, u32[]{:S(2)}) copy-start(f32[2,4]{1,0:T(2,128)} %get-tuple-element.83) | copy-start | bytes 100
  661.9 90.8 %copy-start.34 = (f32[2,4]{1,0:T(2,128)S(1)}, f32[2,4]{1,0:T(2,128)}, u32[]{:S(2)}) copy-start(f32[2,4]{1,0:T(2,128)} %get-tuple-element.81) | copy-start | bytes 100
  661.9 241.9 %copy-start.47 = (f32[1024]{0:T(1024)S(1)}, f32[1024]{0:T(1024)}, u32[]{:S(2)}) copy-start(f32[1024]{0:T(1024)} %param.39) | copy-start | bytes 12292
  661.9 445.6 %reduce-scatter.15.cloned.1.call-start = ((), (), s32[]{:S(2)}) async-start(), calls=%async_computation.21 | async-start | bytes 327680 | tf_op jit(solution)/shard_map/reduce_scatter | solution.py:250
  662.6 446.4 %reduce-scatter.11.cloned.1.call-start = ((), (), s32[]{:S(2)}) async-start(), calls=%async_computation.19 | async-start | bytes 983040 | tf_op jit(solution)/shard_map/reduce_scatter | solution.py:247
  751.9 379.3 %reduce-scatter.23.cloned.1.call-start = ((), (), s32[]{:S(2)}) async-start(), calls=%async_computation.25 | async-start | bytes 1310720 | tf_op jit(solution)/shard_map/reduce_scatter | solution.py:256
  903.7 34.6 %copy-start.19 = (bf16[128,768]{1,0:T(8,128)(2,1)S(1)}, bf16[128,768]{1,0:T(8,128)(2,1)}, u32[]{:S(2)}) copy-start(bf16[128,768]{1,0:T(8,128)(2,1)} %param.30) | copy-start | bytes 589828
  903.8 255.0 %reduce-scatter.19.cloned.1.call-start = ((), (), s32[]{:S(2)}) async-start(), calls=%async_computation.23 | async-start | bytes 1310720 | tf_op jit(solution)/shard_map/reduce_scatter | solution.py:253
  (40 other events, 246.5 us)
Sparse Core Ops, SparseCore 0:
  9.6 20.8 all-gather.10
  32.0 16.8 all-gather.14
  51.1 99.0 all-gather.6
  152.2 47.6 all-gather.8
  201.8 123.4 all-gather.12
  327.2 123.0 all-gather.16
  486.9 66.2 reduce-scatter.12
  636.6 115.1 reduce-scatter.8
  755.5 148.1 reduce-scatter.20
  907.6 148.2 reduce-scatter.16
  1058.4 19.0 reduce-scatter.14
  1080.1 23.4 reduce-scatter.10
  1106.1 25.0 reduce-scatter.22
  1133.8 24.9 reduce-scatter.18
where the time goes:
time: 1170 us
  waiting for transfers between devices  725 us (62%)
  blocking collectives  154 us (13%)
  matrix products  153 us (13%)
  local copies, waits for them, and re-layouts  71.4 us (6%)
  other arithmetic  39.2 us (3%)
  between operations  15.3 us (1%)
    reduce_scatter x1, waiting for transfers between devices, body(): lax.psum_scatter(grad_contract.astype(jnp.bfloat16), 'fsdp', scatter_dime...  151 us
    all_gather x1, waiting for transfers between devices, body(): lax.all_gather(partial_full[3], 'fsdp', axis=0, tiled=True)  115 us
    reduce_scatter x1, waiting for transfers between devices, body(): lax.psum_scatter(grad_expand.astype(jnp.bfloat16), 'fsdp', scatter_dimens...  105 us
    all_gather x1, waiting for transfers between devices, body(): lax.all_gather(partial_full[0], 'fsdp', axis=0, tiled=True)  101 us
    reduce_scatter x1, waiting for transfers between devices, body(): lax.psum_scatter(grad_mixing.astype(jnp.bfloat16), 'fsdp', scatter_dimens...  89.2 us
    all_to_all x1, blocking collectives, body(): lax.all_to_all(packed_cot, 'seq', split_axis=1, concat_axis=2, tiled=True)  53.8 us
    all_gather x1, waiting for transfers between devices, body(): lax.all_gather(partial_full[2], 'fsdp', axis=0, tiled=True)  48.9 us
    psum x1, blocking collectives, body(): lax.psum((grad_first_gain, grad_first_shift, grad_mixing_bias, grad_outpu...  40.8 us
  transfers between devices with their start and end apart: 16, of which 12 were waited for; matrix products, arithmetic and copies ran while one was open for 19% of the time, Pallas kernels for 0%

commit v1 on v0

v1 whole, which is shorter than its diff:
```python
import functools
import math

import jax
import jax.numpy as jnp
from jax import lax
from jax.experimental import pallas as pl
from jax.experimental.pallas import tpu as pltpu
from jax.sharding import PartitionSpec as P

HEAD = 64
LOG2E = math.log2(math.e)
BF = jnp.bfloat16
F32 = jnp.float32


def swap(value, axis, size, bit):
    return lax.ppermute(value, axis, [(i, i ^ bit) for i in range(size)])


def bits_of(size):
    return [1 << p for p in range(size.bit_length() - 1)]


def gather_slots(value, axis, size):
    slots = {0: value}
    for bit in reversed(bits_of(size)):
        for k in list(slots):
            slots[k | bit] = swap(slots[k], axis, size, bit)
    return [slots[k] for k in range(size)]


def scatter_slots(partial, axis, size):
    for bit in bits_of(size):
        pairs = partial.reshape(-1, 2, *partial.shape[1:])
        came = swap(pairs[:, 1].astype(BF), axis, size, bit)
        partial = pairs[:, 0] + came.astype(F32)
    return partial[0]


def gather_rows(value, index, axis, size):
    value = value[None]
    for bit in reversed(bits_of(size)):
        came = swap(value, axis, size, bit)
        value = jnp.where(
            (index & bit) != 0,
            jnp.stack([came, value], axis=1),
            jnp.stack([value, came], axis=1),
        ).reshape(-1, *value.shape[1:])
    return value


def scatter_rows(value, index, axis, size):
    for bit in bits_of(size):
        pairs = value.reshape(-1, 2, *value.shape[1:])
        own = ((index & bit) != 0).astype(jnp.int32)
        sent = lax.dynamic_index_in_dim(pairs, 1 - own, 1, keepdims=False).astype(BF)
        kept = lax.dynamic_index_in_dim(pairs, own, 1, keepdims=False).astype(F32)
        value = kept + swap(sent, axis, size, bit).astype(F32)
    return value[0]


def exchange_slots(slots, axis, size):
    return [slots[0]] + [swap(slots[k], axis, size, k) for k in range(1, size)]


def all_sum(value, axes):
    for axis, size in axes:
        for bit in bits_of(size):
            value = value + swap(value, axis, size, bit)
    return value


def dot(a, b, dims):
    return lax.dot_general(a, b, (dims, ((), ())), preferred_element_type=F32)


def head_mask(width, head):
    lanes = lax.broadcasted_iota(jnp.int32, (1, width), 1)
    return (lanes // HEAD) == head


def causal(tile):
    keys = lax.broadcasted_iota(jnp.int32, (tile, tile), 0)
    queries = lax.broadcasted_iota(jnp.int32, (tile, tile), 1)
    return keys <= queries


def forward_kernel(slots, tile, width, at_ref, q_ref, k_ref, v_ref, o_ref, lse_ref, peak_ref, k_s, vt_s):
    here = at_ref[0]
    scale = HEAD**-0.5
    factor = scale * LOG2E
    heads = width // HEAD
    for i in range(slots):
        rows = slice(i * tile, (i + 1) * tile)
        k_s[rows, :] = k_ref[i ^ here]
        vt_s[:, rows] = v_ref[i ^ here].T

    def scores(q, start, stop, masked):
        found = dot(k_s[start:stop], q, ((1,), (1,)))
        if masked:
            edge = jnp.where(causal(tile), found[stop - start - tile :], -jnp.inf)
            if stop - start == tile:
                return edge
            return jnp.concatenate([found[: stop - start - tile], edge], axis=0)
        return found

    peaks = [None] * heads
    for i in range(slots):
        q_tile = q_ref[i ^ here]
        outs = []
        for h in range(heads):
            q = jnp.where(head_mask(width, h), q_tile, jnp.zeros_like(q_tile))
            top = total = acc = None
            limit = (i + 1) * tile
            step = min(limit, 4 * tile)
            for start in range(0, limit, step):
                stop = min(start + step, limit)
                found = scores(q, start, stop, stop == limit)
                high = jnp.max(found, axis=0, keepdims=True)
                new_top = high if top is None else jnp.maximum(top, high)
                grown = jnp.exp2((found - new_top) * factor)
                part = jnp.sum(grown, axis=0, keepdims=True)
                mixed = dot(
                    vt_s[h * HEAD : (h + 1) * HEAD, start:stop], grown.astype(BF), ((1,), (0,))
                )
                if top is None:
                    total, acc = part, mixed
                else:
                    shrink = jnp.exp2((top - new_top) * factor)
                    total = total * shrink + part
                    acc = acc * shrink + mixed
                top = new_top
            outs.append(acc / total)
            lse_ref[h : h + 1, i * tile : (i + 1) * tile] = top * factor + jnp.log2(total)
            peaks[h] = top if peaks[h] is None else jnp.maximum(peaks[h], top)
        joined = outs[0] if heads == 1 else jnp.concatenate(outs, axis=0)
        o_ref[i ^ here] = joined.T.astype(BF)
    for h in range(heads):
        peak_ref[h : h + 1, :] = peaks[h] * scale


def backward_kernel(
    slots, tile, width, at_ref, q_ref, k_ref, v_ref, o_ref, g_ref, lse_ref, dq_ref, dk_ref, dv_ref,
    k_s, v_s, kt_s, dk_s, dv_s,
):
    here = at_ref[0]
    scale = HEAD**-0.5
    factor = scale * LOG2E
    heads = width // HEAD
    for i in range(slots):
        rows = slice(i * tile, (i + 1) * tile)
        k_s[rows, :] = k_ref[i ^ here]
        v_s[rows, :] = v_ref[i ^ here]
        kt_s[:, rows] = k_ref[i ^ here].T
    for i in reversed(range(slots)):
        q_tile = q_ref[i ^ here]
        g_tile = g_ref[i ^ here]
        inner = (g_tile.astype(F32) * o_ref[i ^ here].astype(F32)).T
        outs = []
        limit = (i + 1) * tile
        for h in range(heads):
            mask = head_mask(width, h)
            q = jnp.where(mask, q_tile, jnp.zeros_like(q_tile))
            g = jnp.where(mask, g_tile, jnp.zeros_like(g_tile))
            delta = jnp.sum(inner[h * HEAD : (h + 1) * HEAD], axis=0, keepdims=True)
            lse = lse_ref[h : h + 1, i * tile : (i + 1) * tile]
            acc = None
            step = min(limit, 4 * tile)
            for start in range(0, limit, step):
                stop = min(start + step, limit)
                found = dot(k_s[start:stop], q, ((1,), (1,)))
                probs = jnp.exp2(found * factor - lse)
                if stop == limit:
                    edge = jnp.where(causal(tile), probs[stop - start - tile :], 0.0)
                    if stop - start == tile:
                        probs = edge
                    else:
                        probs = jnp.concatenate([probs[: stop - start - tile], edge], axis=0)
                spread = dot(v_s[start:stop], g, ((1,), (1,)))
                logit_cot = (probs * (spread - delta)).astype(BF)
                dv_part = dot(probs.astype(BF), g, ((1,), (0,)))
                dk_part = dot(logit_cot, q, ((1,), (0,)))
                if i == slots - 1 and h == 0:
                    dv_s[start:stop] = dv_part
                    dk_s[start:stop] = dk_part
                else:
                    dv_s[start:stop] += dv_part
                    dk_s[start:stop] += dk_part
                dq_part = dot(kt_s[h * HEAD : (h + 1) * HEAD, start:stop], logit_cot, ((1,), (0,)))
                acc = dq_part if acc is None else acc + dq_part
            outs.append(acc)
        joined = outs[0] if heads == 1 else jnp.concatenate(outs, axis=0)
        dq_ref[i ^ here] = (joined.T * scale).astype(BF)
    for i in range(slots):
        rows = slice(i * tile, (i + 1) * tile)
        dk_ref[i ^ here] = (dk_s[rows] * scale).astype(BF)
        dv_ref[i ^ here] = dv_s[rows].astype(BF)


def part_specs(mixed, width, groups):
    slots, tile, columns = mixed.shape
    every = columns // 3
    if width % 128 == 0:
        return [mixed] * 3, [
            pl.BlockSpec((slots, tile, width), lambda g, at, j=j: (0, 0, j * groups + g))
            for j in range(3)
        ]
    pieces = [mixed[..., j * every : (j + 1) * every] for j in range(3)]
    return pieces, [pl.BlockSpec((slots, tile, width), lambda g, at: (0, 0, g))] * 3


def group_width(mixed):
    every = mixed.shape[-1] // 3
    width = 128 if every % 128 == 0 else every
    return every, width, every // width


def attend_forward(at, mixed):
    slots, tile, _ = mixed.shape
    every, width, groups = group_width(mixed)
    heads = width // HEAD
    length = slots * tile
    operands, specs = part_specs(mixed, width, groups)
    out, lse, peak = pl.pallas_call(
        functools.partial(forward_kernel, slots, tile, width),
        out_shape=(
            jax.ShapeDtypeStruct((slots, tile, every), BF),
            jax.ShapeDtypeStruct((groups, heads, length), F32),
            jax.ShapeDtypeStruct((groups, heads, tile), F32),
        ),
        grid_spec=pltpu.PrefetchScalarGridSpec(
            num_scalar_prefetch=1,
            grid=(groups,),
            in_specs=specs,
            out_specs=(
                pl.BlockSpec((slots, tile, width), lambda g, at: (0, 0, g)),
                pl.BlockSpec((None, heads, length), lambda g, at: (g, 0, 0)),
                pl.BlockSpec((None, heads, tile), lambda g, at: (g, 0, 0)),
            ),
            scratch_shapes=[pltpu.VMEM((length, width), BF), pltpu.VMEM((width, length), BF)],
        ),
        compiler_params=pltpu.CompilerParams(vmem_limit_bytes=40 << 20),
        cost_estimate=pl.CostEstimate(
            flops=2 * length * length * every * 4,
            transcendentals=length * length * every // HEAD // 2,
            bytes_accessed=8 * length * every,
        ),
        name="attend_forward",
    )(at, *operands)
    return out, lse, jnp.max(peak, axis=-1).reshape(-1)


def attend_backward(at, mixed, out, cot, lse):
    slots, tile, _ = mixed.shape
    every, width, groups = group_width(mixed)
    heads = width // HEAD
    length = slots * tile
    operands, specs = part_specs(mixed, width, groups)
    block = pl.BlockSpec((slots, tile, width), lambda g, at: (0, 0, g))
    shape = jax.ShapeDtypeStruct((slots, tile, every), BF)
    return pl.pallas_call(
        functools.partial(backward_kernel, slots, tile, width),
        out_shape=(shape, shape, shape),
        grid_spec=pltpu.PrefetchScalarGridSpec(
            num_scalar_prefetch=1,
            grid=(groups,),
            in_specs=specs
            + [block, block, pl.BlockSpec((None, heads, length), lambda g, at: (g, 0, 0))],
            out_specs=(block, block, block),
            scratch_shapes=[
                pltpu.VMEM((length, width), BF),
                pltpu.VMEM((length, width), BF),
                pltpu.VMEM((width, length), BF),
                pltpu.VMEM((length, width), F32),
                pltpu.VMEM((length, width), F32),
            ],
        ),
        compiler_params=pltpu.CompilerParams(vmem_limit_bytes=40 << 20),
        cost_estimate=pl.CostEstimate(
            flops=2 * length * length * every * 10,
            transcendentals=length * length * every // HEAD // 2,
            bytes_accessed=16 * length * every,
        ),
        name="attend_backward",
    )(at, *operands, out, cot, lse)


def norm_stats(values):
    centered = values - jnp.mean(values, axis=-1, keepdims=True)
    rate = lax.rsqrt(jnp.mean(centered * centered, axis=-1, keepdims=True) + 1e-05)
    return centered * rate, rate


def norm_back(cot, unit, rate, gain):
    e = cot * gain
    return rate * (
        e
        - jnp.mean(e, axis=-1, keepdims=True)
        - unit * jnp.mean(e * unit, axis=-1, keepdims=True)
    )


def gelu_pair(v):
    k0 = math.sqrt(2.0 / math.pi)
    square = v * v
    t = jnp.tanh(k0 * v * (1.0 + 0.044715 * square))
    half = 0.5 * (1.0 + t)
    slope = half + 0.5 * v * (1.0 - t * t) * (k0 * (1.0 + 3.0 * 0.044715 * square))
    return v * half, slope


def body(
    n, shards,
    tokens, first_gain, first_shift, attention_weight, attention_bias, output_weight, output_bias,
    second_gain, second_shift, expand_weight, expand_bias, contract_weight, contract_bias,
    cotangent, threshold,
):
    batch, tile, width = tokens.shape
    rows, qkv = attention_weight.shape
    every = qkv // 3
    heads = every // HEAD
    inner_rows = contract_weight.shape[0]
    inner = inner_rows * shards // n
    piece = inner_rows // n
    ratio = shards // n
    strip = output_weight.shape[1]
    s = lax.axis_index("seq")
    f = lax.axis_index("fsdp")
    at = s.astype(jnp.int32).reshape(1)

    def by_kind(v):
        lead = v.shape[:-1]
        return jnp.swapaxes(v.reshape(*lead, heads, 3, HEAD), -3, -2).reshape(*lead, qkv)

    def by_head(v):
        lead = v.shape[:-1]
        return jnp.swapaxes(v.reshape(*lead, 3, heads, HEAD), -3, -2).reshape(*lead, qkv)

    mixing = gather_rows(by_kind(attention_weight), f, "fsdp", shards).reshape(width, qkv)
    to_seq = jnp.concatenate(
        [
            jnp.swapaxes(expand_weight.reshape(rows, ratio, n, piece), 1, 2)
            .swapaxes(0, 1)
            .reshape(n, -1, strip),
            contract_weight.reshape(n, piece, strip),
            jnp.broadcast_to(output_weight[None], (n, rows, strip)),
        ],
        axis=1,
    )
    from_seq = lax.all_to_all(to_seq, "seq", 0, 0, tiled=True)
    cut = rows * ratio * piece // strip
    expand_rows = (
        from_seq[:, :cut].reshape(n, rows, ratio * piece).swapaxes(0, 1).reshape(rows, inner)
    )
    contract_rows = from_seq[:, cut : cut + piece].swapaxes(0, 1).reshape(piece, width)
    output_rows = from_seq[:, cut + piece :].swapaxes(0, 1).reshape(rows, width)
    output_full = gather_rows(output_rows, f, "fsdp", shards).reshape(n, every, width)
    output_full = jnp.concatenate(
        [lax.dynamic_index_in_dim(output_full, s ^ k, 0, keepdims=False) for k in range(n)]
    )
    if piece == rows:
        both = gather_rows(jnp.stack([expand_rows, contract_rows]), f, "fsdp", shards)
        expand = both[:, 0].reshape(width, inner)
        contract = both[:, 1].reshape(inner, width)
    else:
        expand = gather_rows(expand_rows, f, "fsdp", shards).reshape(width, inner)
        contract = gather_rows(contract_rows, f, "fsdp", shards).reshape(inner, width)

    mixing_bias = by_kind(lax.dynamic_slice_in_dim(attention_bias, s * qkv, qkv))
    inner_bias = lax.dynamic_index_in_dim(
        expand_bias.reshape(shards, n, piece), s, axis=1, keepdims=False
    ).reshape(inner)

    streams = range(batch)
    first_unit, first_rate, normed_first, mixed, attended_own, lse, peaks = ([None] * batch for _ in range(7))
    attended, residual = [None] * batch, [None] * batch
    second_unit, second_rate, normed_second = ([None] * batch for _ in range(3))
    cot_all = [None] * batch
    for b in streams:
        first_unit[b], first_rate[b] = norm_stats(tokens[b].astype(F32))
        own = (first_unit[b] * first_gain + first_shift).astype(BF)
        normed_first[b] = jnp.concatenate(gather_slots(own, "seq", n), axis=0)
    for b in streams:
        cot_all[b] = jnp.concatenate(gather_slots(cotangent[b], "seq", n), axis=0)
    for b in streams:
        mixed[b] = (
            (dot(normed_first[b], mixing, ((1,), (0,))) + mixing_bias)
            .astype(BF)
            .reshape(n, tile, qkv)
        )
        attended_own[b], lse[b], peaks[b] = attend_forward(at, mixed[b])
        attended[b] = jnp.concatenate(
            exchange_slots([attended_own[b][k] for k in range(n)], "seq", n), axis=-1
        )
    for b in streams:
        residual[b] = (
            tokens[b].astype(F32) + dot(attended[b], output_full, ((1,), (0,))) + output_bias
        )
        second_unit[b], second_rate[b] = norm_stats(residual[b])
        own = (second_unit[b] * second_gain + second_shift).astype(BF)
        normed_second[b] = jnp.concatenate(gather_slots(own, "seq", n), axis=0)

    active, hidden_cot, residual_cot, block_output = ([None] * batch for _ in range(4))
    branch_cot, heads_cot = [None] * batch, [None] * batch
    gains = []
    for b in streams:
        hidden = dot(normed_second[b], expand, ((1,), (0,))) + inner_bias
        value, slope = gelu_pair(hidden)
        active[b] = value.astype(BF)
        hidden_cot[b] = (dot(cot_all[b], contract, ((1,), (1,))) * slope).astype(BF)
        partial = dot(hidden_cot[b], expand, ((1,), (1,))).reshape(n, tile, width)
        second_cot = scatter_slots(partial, "seq", n)
        residual_cot[b] = cotangent[b].astype(F32) + norm_back(
            second_cot, second_unit[b], second_rate[b], second_gain
        )
        branch_cot[b] = residual_cot[b].astype(BF)
        gains.append(
            (
                jnp.sum(second_cot * second_unit[b], axis=0),
                jnp.sum(second_cot, axis=0),
                jnp.sum(branch_cot[b].astype(F32), axis=0),
                jnp.sum(cotangent[b].astype(F32), axis=0),
                jnp.sum(hidden_cot[b].astype(F32), axis=0),
            )
        )
        own_cot = dot(branch_cot[b], output_full, ((1,), (1,))).astype(BF)
        heads_cot[b] = jnp.stack(
            exchange_slots([own_cot[:, k * every : (k + 1) * every] for k in range(n)], "seq", n)
        )
    for b in streams:
        partial_out = dot(active[b], contract, ((1,), (0,))).reshape(n, tile, width)
        total = scatter_slots(partial_out, "seq", n)
        block_output[b] = (residual[b] + total + contract_bias).astype(BF)

    def over_streams(left, right):
        return functools.reduce(
            jnp.add, [dot(left[b], right[b], ((0,), (0,))) for b in streams]
        )

    def reduce_rows(grad):
        return scatter_rows(grad.reshape(shards, -1, grad.shape[-1]), f, "fsdp", shards)

    if piece == rows:
        joined = jnp.stack(
            [
                over_streams(normed_second, hidden_cot).astype(BF).reshape(shards, rows, inner),
                over_streams(active, cot_all).astype(BF).reshape(shards, piece, width),
            ],
            axis=1,
        )
        grad_expand, grad_contract = scatter_rows(joined, f, "fsdp", shards)
    else:
        grad_expand = reduce_rows(over_streams(normed_second, hidden_cot))
        grad_contract = reduce_rows(over_streams(active, cot_all))
    by_slot = over_streams(attended, branch_cot).astype(BF).reshape(n, every, width)
    grad_output = reduce_rows(
        jnp.concatenate(
            [lax.dynamic_index_in_dim(by_slot, s ^ k, 0, keepdims=False) for k in range(n)]
        )
    )
    back = lax.all_to_all(
        jnp.concatenate(
            [
                grad_expand.astype(BF)
                .reshape(rows, n, ratio * piece)
                .swapaxes(0, 1)
                .reshape(n, cut, strip),
                grad_contract.astype(BF).reshape(piece, n, strip).swapaxes(0, 1),
            ],
            axis=1,
        ),
        "seq",
        0,
        0,
        tiled=True,
    )
    grad_expand_own = (
        back[:, :cut]
        .reshape(n, rows, ratio, piece)
        .transpose(1, 2, 0, 3)
        .reshape(rows, ratio * n * piece)
        .astype(F32)
    )
    grad_contract_own = back[:, cut:].reshape(inner_rows, strip).astype(F32)
    grad_output_own = scatter_rows(
        grad_output.reshape(rows, n, strip).swapaxes(0, 1), s, "seq", n
    )

    mixed_cot, input_grad = [None] * batch, [None] * batch
    tail = []
    for b in streams:
        parts = attend_backward(at, mixed[b], attended_own[b], heads_cot[b], lse[b])
        mixed_cot[b] = jnp.concatenate(parts, axis=-1).reshape(n * tile, qkv)
        partial = dot(mixed_cot[b], mixing, ((1,), (1,))).reshape(n, tile, width)
        first_cot = scatter_slots(partial, "seq", n)
        input_grad[b] = residual_cot[b] + norm_back(
            first_cot, first_unit[b], first_rate[b], first_gain
        )
        tail.append(
            (
                jnp.sum(first_cot * first_unit[b], axis=0),
                jnp.sum(first_cot, axis=0),
                jnp.sum(mixed_cot[b].astype(F32), axis=0),
            )
        )
    grad_mixing = by_head(reduce_rows(over_streams(normed_first, mixed_cot).astype(BF)))

    axes = (("seq", n), ("fsdp", shards))
    mine = (jnp.arange(n) == s).astype(F32)
    second_gain_sum, second_shift_sum, output_sum, contract_sum, inner_sum = (
        functools.reduce(jnp.add, [g[j] for g in gains]) for j in range(5)
    )
    spread_inner = (inner_sum.reshape(shards, 1, piece) * mine[None, :, None]).reshape(-1)
    early = all_sum(
        jnp.concatenate(
            [second_gain_sum, second_shift_sum, output_sum, contract_sum, spread_inner]
        ).reshape(-1, 128),
        axes,
    ).reshape(-1)
    first_gain_sum, first_shift_sum, mixing_sum = (
        functools.reduce(jnp.add, [g[j] for g in tail]) for j in range(3)
    )
    spread_mixing = (mine[:, None] * by_head(mixing_sum)[None]).reshape(-1)
    late = all_sum(
        jnp.concatenate([first_gain_sum, first_shift_sum, spread_mixing]).reshape(-1, 128), axes
    ).reshape(-1)

    head_peak = functools.reduce(jnp.maximum, peaks)
    for bit in bits_of(shards):
        head_peak = jnp.maximum(head_peak, swap(head_peak, "fsdp", shards, bit))
    factor = jnp.sqrt(threshold[0] / jnp.maximum(head_peak, threshold[0]))
    multiplier = jnp.broadcast_to(
        jnp.stack([factor, factor, jnp.ones_like(factor)], axis=1)[:, :, None], (heads, 3, HEAD)
    ).reshape(qkv)
    clipped_weight = attention_weight.astype(F32) * multiplier[None, :]
    clipped_bias = lax.dynamic_slice_in_dim(attention_bias, s * qkv, qkv) * multiplier

    return (
        jnp.stack(block_output),
        jnp.stack(input_grad),
        late[:width],
        late[width : 2 * width],
        grad_mixing,
        late[2 * width :],
        grad_output_own,
        early[2 * width : 3 * width],
        early[:width],
        early[width : 2 * width],
        grad_expand_own,
        early[4 * width :],
        grad_contract_own,
        early[3 * width : 4 * width],
        head_peak,
        clipped_weight,
        clipped_bias,
    )


def solution(mesh):
    grid, both, whole, line = P("fsdp", "seq"), P("fsdp", "seq", None), P(), P("seq")
    return jax.shard_map(
        functools.partial(body, mesh.shape["seq"], mesh.shape["fsdp"]),
        mesh=mesh,
        in_specs=(
            both, whole, whole, grid, whole, grid, whole, whole, whole, grid, whole, grid, whole,
            both, whole,
        ),
        out_specs=(
            both, both, whole, whole, grid, whole, grid, whole, whole, whole, grid, whole, grid,
            whole, line, grid, line,
        ),
        check_vma=False,
    )
```

time: 1170 us -> 516 us (0.44)
  waiting for transfers between devices: 725 us -> 202 us
  blocking collectives: 154 us -> 0 us
  matrix products: 153 us -> 79.3 us
  starting transfers between devices: 9.06 us -> 80 us
  Pallas kernels: 0 us -> 33.2 us
  local copies, waits for them, and re-layouts: 71.4 us -> 49.2 us
  other arithmetic: 39.2 us -> 58.2 us
    reduce_scatter x8 -> x0, waiting for transfers between devices: 392 us -> none  [the longest x1 151 us: body(): lax.psum_scatter(grad_contract.astype(jnp.bfloat16), 'fsdp', scatter_dime...]
    all_gather x6 -> x0, waiting for transfers between devices: 284 us -> none  [the longest x1 115 us: body(): lax.all_gather(partial_full[3], 'fsdp', axis=0, tiled=True)]
    ppermute x0 -> x75, waiting for transfers between devices: none -> 195 us  [swap(): return lax.ppermute(value, axis, [(i, i ^ bit) for i in range(size)])]
    dot_general x24, matrix products: 153 us -> 79.3 us  [dot(): return lax.dot_general(a, b, (dims, ((), ())), preferred_element_type=F32)]
    all_to_all x2 -> x0, blocking collectives: 72.7 us -> none  [the longest x1 53.8 us: body(): lax.all_to_all(packed_cot, 'seq', split_axis=1, concat_axis=2, tiled=True)]
    ppermute x0 -> x75, starting transfers between devices: none -> 72.2 us  [swap(): return lax.ppermute(value, axis, [(i, i ^ bit) for i in range(size)])]
    psum x1 -> x0, blocking collectives: 40.8 us -> none  [body(): lax.psum((grad_first_gain, grad_first_shift, grad_mixing_bias, grad_outpu...]
    all_to_all x2, waiting for transfers between devices: 46.4 us -> 7.54 us  [the longest x1 7.54 us: body(): lax.all_to_all(jnp.concatenate([grad_expand.astype(BF).reshape(rows, n, r...]
  transfers between devices with their start and end apart: 16 -> 77, of which waited for: 12 -> 29; matrix products, arithmetic and copies ran while one was open for 19% -> 35% of each run, Pallas kernels for 0% -> 7%
where the time goes in v1:
time: 516 us; the launch traced here: 506 us
  waiting for transfers between devices  202 us (39%)
  starting transfers between devices  80 us (16%)
  matrix products  79.3 us (15%)
  other arithmetic  58.2 us (11%)
  local copies, waits for them, and re-layouts  49.2 us (10%)
  Pallas kernels  33.2 us (6%)
    ppermute x75, waiting for transfers between devices, swap(): return lax.ppermute(value, axis, [(i, i ^ bit) for i in range(size)])  195 us
    dot_general x24, matrix products, dot(): return lax.dot_general(a, b, (dims, ((), ())), preferred_element_type=F32)  79.3 us
    ppermute x75, starting transfers between devices, swap(): return lax.ppermute(value, axis, [(i, i ^ bit) for i in range(size)])  72.2 us
    select_n x12, other arithmetic, gather_rows(): jnp.where(index & bit != 0, jnp.stack([came, value], axis=1), jnp.stack([...  19.8 us
    pallas_call x2, Pallas kernels, attend_forward(): pl.pallas_call(functools.partial(forward_kernel, slots, tile, width), out...  16.8 us
    pallas_call x2, Pallas kernels, attend_backward(): pl.pallas_call(functools.partial(backward_kernel, slots, tile, width), ou...  16.4 us
  transfers between devices with their start and end apart: 77, of which 29 were waited for; matrix products, arithmetic and copies ran while one was open for 35% of the time, Pallas kernels for 7%

profile of v1, /device:TPU:0, one launch (start us, length us, event | category | flops | bytes accessed | tf_op | source)
XLA Modules:
  0.0 505.9 jit_solution(5096842070923702883)
XLA Ops:
  5.0 4.3 all-to-all-start
  21.1 5.9 %collective-permute-done.3 = bf16[1,128,768]{1,2,0:T(8,128)(2,1)S(1)} collective-permute-done((bf16[1,128,768]{1,2,0:T(8,128)(2,1)S(1)}, bf16[1,128,768]{1,2,0:T(8,128)(2,1)S(1)}, u32[]{:S(2)}, u32[]{:S(2)}) %collective-permute-start.3) | collective-permute-done | bytes 196640 | tf_op jit(solution)/shard_map/ppermute | solution.py:18
  33.2 10.9 %collective-permute-done.4 = bf16[2,128,768]{1,2,0:T(8,128)(2,1)S(1)} collective-permute-done((bf16[2,128,768]{1,2,0:T(8,128)(2,1)S(1)}, bf16[2,128,768]{1,2,0:T(8,128)(2,1)S(1)}, u32[]{:S(2)}, u32[]{:S(2)}) %collective-permute-start.4) | collective-permute-done | bytes 393248 | tf_op jit(solution)/shard_map/ppermute | solution.py:18
  50.5 17.1 %collective-permute-done.9 = bf16[1,128,1024]{1,2,0:T(8,128)(2,1)S(1)} collective-permute-done((bf16[1,128,1024]{1,2,0:T(8,128)(2,1)S(1)}, bf16[1,128,1024]{1,2,0:T(8,128)(2,1)S(1)}, u32[]{:S(2)}, u32[]{:S(2)}) %collective-permute-start.9) | collective-permute-done | bytes 262176 | tf_op jit(solution)/shard_map/ppermute | solution.py:18
  79.0 8.3 %attend_forward.2 = (bf16[4,256,256]{2,1,0:T(8,128)(2,1)S(1)}, f32[2,2,1024]{2,1,0:T(2,128)S(1)}, f32[2,2,256]{2,1,0:T(2,128)S(1)}) custom-call(s32[1]{0:T(128)} %bitcast.1.at_ref, bf16[4,256,768]{2,1,0:T(8,128)(2,1)S(1)} %bitcast.550, bf16[4,256,768]{2,1,0:T(8,128)(2,1)S(1)} %bitcast.551, bf16[4,256,768]{2,1,0:T(8,128)(2,1)S(1)} %bitcast.552), custom_call_target="tpu_custom_call" | custom-call | flops 2147483648 | bytes 2097152 | tf_op jit(solution)/shard_map/attend_forward/pallas_call | solution.py:225
  96.9 8.5 %attend_forward.3 = (bf16[4,256,256]{2,1,0:T(8,128)(2,1)S(1)}, f32[2,2,1024]{2,1,0:T(2,128)S(1)}, f32[2,2,256]{2,1,0:T(2,128)S(1)}) custom-call(s32[1]{0:T(128)} %bitcast.1.at_ref, bf16[4,256,768]{2,1,0:T(8,128)(2,1)S(1)} %bitcast.544, bf16[4,256,768]{2,1,0:T(8,128)(2,1)S(1)} %bitcast.545, bf16[4,256,768]{2,1,0:T(8,128)(2,1)S(1)} %bitcast.546), custom_call_target="tpu_custom_call" | custom-call | flops 2147483648 | bytes 2097152 | tf_op jit(solution)/shard_map/attend_forward/pallas_call | solution.py:225
  106.2 10.0 %collective-permute-done.72 = f32[4]{0:T(128)S(1)} collective-permute-done((f32[4]{0:T(128)S(1)}, f32[4]{0:T(128)S(1)}, u32[]{:S(2)}, u32[]{:S(2)}) %collective-permute-start.72) | collective-permute-done | bytes 48 | tf_op jit(solution)/shard_map/ppermute | solution.py:18
  149.0 10.3 %collective-permute-done.27 = bf16[256,1024]{1,0:T(8,128)(2,1)} collective-permute-done((bf16[256,1024]{1,0:T(8,128)(2,1)}, bf16[256,1024]{1,0:T(8,128)(2,1)}, u32[]{:S(2)}, u32[]{:S(2)}) %collective-permute-start.27) | collective-permute-done | bytes 524320 | tf_op jit(solution)/shard_map/ppermute | solution.py:18
  161.0 23.4 %collective-permute-done.17 = bf16[4,2,128,1024]{2,3,1,0:T(8,128)(2,1)} collective-permute-done((bf16[4,2,128,1024]{2,3,1,0:T(8,128)(2,1)}, bf16[4,2,128,1024]{2,3,1,0:T(8,128)(2,1)}, u32[]{:S(2)}, u32[]{:S(2)}) %collective-permute-start.17) | collective-permute-done | bytes 2097184 | tf_op jit(solution)/shard_map/ppermute | solution.py:18
  184.3 5.8 %maximum_select_fusion = bf16[4,2,2,128,1024]{3,4,2,0,1:T(8,128)(2,1)} fusion(bf16[4,1,2,128,1024]{3,4,2,0,1:T(8,128)(2,1)} %bitcast.48, bf16[4,1,2,128,1024]{3,4,2,0,1:T(8,128)(2,1)} %bitcast.47, pred[]{:T(512)S(6)} %ne.10), kind=kLoop, calls=%fused_computation.4 | loop fusion | flops 6291456 | bytes 8388609 | tf_op jit(solution)/shard_map/jit(_where)/select_n | solution.py:45
  190.1 6.3 %copy.183 = bf16[4,2,2,128,1024]{4,3,1,0,2:T(8,128)(2,1)} copy(bf16[4,2,2,128,1024]{3,4,2,0,1:T(8,128)(2,1)} %maximum_select_fusion) | data formatting | bytes 8388608 | tf_op jit(solution)/shard_map/jit(_where)/select_n | solution.py:45
  201.7 3.9 fusion.99
  205.9 7.9 %collective-permute-done.32 = bf16[256,1024]{1,0:T(8,128)(2,1)S(1)} collective-permute-done((bf16[256,1024]{1,0:T(8,128)(2,1)S(1)}, bf16[256,1024]{1,0:T(8,128)(2,1)S(1)}, u32[]{:S(2)}, u32[]{:S(2)}) %collective-permute-start.32) | collective-permute-done | bytes 524320 | tf_op jit(solution)/shard_map/ppermute | solution.py:18
  214.3 7.7 %multiply_convert_fusion.3 = (bf16[1024,1024]{1,0:T(8,128)(2,1)S(1)}, bf16[1024,1024]{1,0:T(8,128)(2,1)S(1)}, f32[1024,1024]{1,0:T(8,128)S(1)}) fusion(f32[1024]{0:T(1024)S(1)} %bitcast.624, f32[1024,1024]{1,0:T(8,128)S(1)} %fusion.99, bf16[1024,1024]{1,0:T(8,128)(2,1)S(1)} %bitcast.580, bf16[256,1024]{1,0:T(8,128)(2,1)S(1)} %collective-permute-done.14, ...), kind=kOutput, calls=%fused_computation.16 | convolution fusion | flops 2176843776 | bytes 16781312 | tf_op jit(solution)/shard_map/dot_general | solution.py:75
  222.1 6.9 %convert_reduce_fusion.1 = (f32[1024]{0:T(1024)S(1)}, bf16[1024,1024]{1,0:T(8,128)(2,1)S(1)}) fusion(f32[1024,1024]{1,0:T(8,128)S(1)} %get-tuple-element.205, f32[1024]{0:T(1024)S(1)} %bitcast.625, bf16[1024,1024]{1,0:T(8,128)(2,1)S(1)} %bitcast.583, bf16[256,1024]{1,0:T(8,128)(2,1)S(1)} %collective-permute-done.33, ...), kind=kOutput, calls=%fused_computation.9 | convolution fusion | flops 2177891328 | bytes 10493952 | tf_op jit(solution)/shard_map/dot_general | solution.py:75
  240.2 7.2 %convert_reduce_fusion = (f32[1024]{0:T(1024)S(1)}, bf16[1024,1024]{1,0:T(8,128)(2,1)S(1)}) fusion(f32[1024,1024]{1,0:T(8,128)S(1)} %copy-done.98, f32[1024]{0:T(1024)S(1)} %bitcast.626, bf16[1024,1024]{1,0:T(8,128)(2,1)S(1)} %bitcast.586, bf16[256,1024]{1,0:T(8,128)(2,1)S(1)} %collective-permute-done.43, bf16[256,1024]{1,0:T(8,128)(2,1)} %collective-permute-done.42, ...), kind=kOutput, calls=%fused_computation.8 | convolution fusion | flops 2177891328 | bytes 10493952 | tf_op jit(solution)/shard_map/dot_general | solution.py:75
  250.5 6.1 %fusion.98 = f32[1024,1024]{1,0:T(8,128)} fusion(bf16[1024,1024]{1,0:T(8,128)(2,1)S(1)} %get-tuple-element.209, bf16[256,1024]{1,0:T(8,128)(2,1)} %collective-permute-done.28, bf16[256,1024]{1,0:T(8,128)(2,1)} %collective-permute-done.27, bf16[256,1024]{1,0:T(8,128)(2,1)} %collective-permute-done.26, bf16[256,1024]{1,0:T(8,128)(2,1)} %get-tuple-element.198), kind=kOutput, calls=%fused_computation.232 | convolution fusion | flops 2155872256 | bytes 8388608 | tf_op jit(solution)/shard_map/dot_general | solution.py:75
  256.6 5.1 %add_convert_fusion.1 = bf16[1024,1024]{1,0:T(8,128)(2,1)S(1)} fusion(f32[1024,1024]{1,0:T(8,128)} %fusion.98, bf16[1024,1024]{1,0:T(8,128)(2,1)S(1)} %copy-done.96, bf16[256,1024]{1,0:T(8,128)(2,1)S(1)} %collective-permute-done.14, bf16[256,1024]{1,0:T(8,128)(2,1)} %collective-permute-done.13, bf16[256,1024]{1,0:T(8,128)(2,1)S(1)} %collective-permute-done.12, ...), kind=kOutput, calls=%fused_computation.7 | convolution fusion | flops 2157969408 | bytes 10485760 | tf_op jit(solution)/shard_map/dot_general | solution.py:75
  261.7 6.0 %fusion.97 = f32[1024,1024]{1,0:T(8,128)} fusion(bf16[1024,1024]{1,0:T(8,128)(2,1)S(1)} %copy-done.94, bf16[256,1024]{1,0:T(8,128)(2,1)S(1)} %collective-permute-done.43, bf16[256,1024]{1,0:T(8,128)(2,1)} %collective-permute-done.42, bf16[256,1024]{1,0:T(8,128)(2,1)} %collective-permute-done.41, bf16[256,1024]{1,0:T(8,128)(2,1)} %get-tuple-element.160), kind=kOutput, calls=%fused_computation.231 | convolution fusion | flops 2155872256 | bytes 8388608 | tf_op jit(solution)/shard_map/dot_general | solution.py:75
  267.7 4.6 add_convert_fusion
  284.6 4.3 collective-permute-done.35
  288.9 11.2 %collective-permute-done.19 = bf16[1,256,1024]{2,1,0:T(8,128)(2,1)S(1)} collective-permute-done((bf16[1,256,1024]{2,1,0:T(8,128)(2,1)S(1)}, bf16[1,256,1024]{2,1,0:T(8,128)(2,1)S(1)}, u32[]{:S(2)}, u32[]{:S(2)}) %collective-permute-start.19) | collective-permute-done | bytes 524320 | tf_op jit(solution)/shard_map/ppermute | solution.py:18
  300.1 11.2 %collective-permute-done.30 = bf16[1,256,1024]{2,1,0:T(8,128)(2,1)S(1)} collective-permute-done((bf16[1,256,1024]{2,1,0:T(8,128)(2,1)S(1)}, bf16[1,256,1024]{2,1,0:T(8,128)(2,1)S(1)}, u32[]{:S(2)}, u32[]{:S(2)}) %collective-permute-start.30) | collective-permute-done | bytes 524320 | tf_op jit(solution)/shard_map/ppermute | solution.py:18
  311.4 10.4 %collective-permute-done.45 = bf16[1,256,1024]{2,1,0:T(8,128)(2,1)S(1)} collective-permute-done((bf16[1,256,1024]{2,1,0:T(8,128)(2,1)S(1)}, bf16[1,256,1024]{2,1,0:T(8,128)(2,1)S(1)}, u32[]{:S(2)}, u32[]{:S(2)}) %collective-permute-start.45) | collective-permute-done | bytes 524320 | tf_op jit(solution)/shard_map/ppermute | solution.py:18
  335.1 5.7 %collective-permute-done.65 = f32[64,128]{1,0:T(8,128)S(1)} collective-permute-done((f32[64,128]{1,0:T(8,128)S(1)}, f32[64,128]{1,0:T(8,128)S(1)}, u32[]{:S(2)}, u32[]{:S(2)}) %collective-permute-start.65) | collective-permute-done | bytes 32800 | tf_op jit(solution)/shard_map/ppermute | solution.py:18
  348.3 8.1 %attend_backward.2 = (bf16[4,256,256]{2,1,0:T(8,128)(2,1)S(1)}, bf16[4,256,256]{2,1,0:T(8,128)(2,1)S(1)}, bf16[4,256,256]{2,1,0:T(8,128)(2,1)S(1)}) custom-call(s32[1]{0:T(128)} %bitcast.1.at_ref, bf16[4,256,768]{2,1,0:T(8,128)(2,1)S(1)} %bitcast.553, bf16[4,256,768]{2,1,0:T(8,128)(2,1)S(1)} %bitcast.554, bf16[4,256,768]{2,1,0:T(8,128)(2,1)S(1)} %bitcast.555, ...), custom_call_target="tpu_custom_call" | custom-call | flops 5368709120 | bytes 4194304 | tf_op jit(solution)/shard_map/attend_backward/pallas_call | solution.py:262
  359.7 8.3 %attend_backward.3 = (bf16[4,256,256]{2,1,0:T(8,128)(2,1)S(1)}, bf16[4,256,256]{2,1,0:T(8,128)(2,1)S(1)}, bf16[4,256,256]{2,1,0:T(8,128)(2,1)S(1)}) custom-call(s32[1]{0:T(128)} %bitcast.1.at_ref, bf16[4,256,768]{2,1,0:T(8,128)(2,1)S(1)} %bitcast.547, bf16[4,256,768]{2,1,0:T(8,128)(2,1)S(1)} %bitcast.548, bf16[4,256,768]{2,1,0:T(8,128)(2,1)S(1)} %bitcast.549, ...), custom_call_target="tpu_custom_call" | custom-call | flops 5368709120 | bytes 4194304 | tf_op jit(solution)/shard_map/attend_backward/pallas_call | solution.py:262
  392.6 6.1 %collective-permute-done.56 = bf16[4,128,768]{2,1,0:T(8,128)(2,1)} collective-permute-done((bf16[4,128,768]{2,1,0:T(8,128)(2,1)}, bf16[4,128,768]{2,1,0:T(8,128)(2,1)}, u32[]{:S(2)}, u32[]{:S(2)}) %collective-permute-start.56) | collective-permute-done | bytes 786464 | tf_op jit(solution)/shard_map/ppermute | solution.py:18
  409.6 16.2 %collective-permute-done.57 = bf16[2,128,768]{2,1,0:T(8,128)(2,1)S(1)} collective-permute-done((bf16[2,128,768]{2,1,0:T(8,128)(2,1)S(1)}, bf16[2,128,768]{2,1,0:T(8,128)(2,1)S(1)}, u32[]{:S(2)}, u32[]{:S(2)}) %collective-permute-start.57) | collective-permute-done | bytes 393248 | tf_op jit(solution)/shard_map/ppermute | solution.py:18
  429.9 9.8 %collective-permute-done.58 = bf16[1,128,768]{2,1,0:T(8,128)(2,1)S(1)} collective-permute-done((bf16[1,128,768]{2,1,0:T(8,128)(2,1)S(1)}, bf16[1,128,768]{2,1,0:T(8,128)(2,1)S(1)}, u32[]{:S(2)}, u32[]{:S(2)}) %collective-permute-start.58) | collective-permute-done | bytes 196640 | tf_op jit(solution)/shard_map/ppermute | solution.py:18
  470.6 13.9 %collective-permute-done.55 = f32[40,128]{1,0:T(8,128)S(1)} collective-permute-done((f32[40,128]{1,0:T(8,128)S(1)}, f32[40,128]{1,0:T(8,128)S(1)}, u32[]{:S(2)}, u32[]{:S(2)}) %collective-permute-start.55) | collective-permute-done | bytes 20512 | tf_op jit(solution)/shard_map/ppermute | solution.py:18
  495.5 7.5 %all-to-all-done.1 = bf16[4,256,256]{1,2,0:T(8,128)(2,1)S(1)} async-done(((bf16[4,256,256]{1,2,0:T(8,128)(2,1)}), bf16[4,256,256]{1,2,0:T(8,128)(2,1)S(1)}, u32[]{:S(2)}, u32[]{:S(2)}) %all-to-all-start.1) | async-done | bytes 524320 | tf_op jit(solution)/shard_map/all_to_all | solution.py:462
  (532 shorter events, 223.2 us)
Async XLA Ops:
  11.5 38.9 %collective-permute-start.1 = (bf16[256,1024]{1,0:T(8,128)(2,1)}, bf16[256,1024]{1,0:T(8,128)(2,1)}, u32[]{:S(2)}, u32[]{:S(2)}) collective-permute-start(bf16[256,1024]{1,0:T(8,128)(2,1)} %get-tuple-element.148), channel_id=1, source_target_pairs={{0,2},{1,3},{2,0},{3,1},{4,6},{5,7},{6,4},{7,5},{8,10},{9,11},{10,... | collective-permute-start | bytes 1572872 | tf_op jit(solution)/shard_map/ppermute | solution.py:18
  13.8 61.2 %collective-permute-start = (bf16[256,1024]{1,0:T(8,128)(2,1)}, bf16[256,1024]{1,0:T(8,128)(2,1)}, u32[]{:S(2)}, u32[]{:S(2)}) collective-permute-start(bf16[256,1024]{1,0:T(8,128)(2,1)} %get-tuple-element.148), channel_id=1, source_target_pairs={{0,1},{1,0},{2,3},{3,2},{4,5},{5,4},{6,7},{7,6},{8,9},{9,8},{10,11... | collective-permute-start | bytes 1572872 | tf_op jit(solution)/shard_map/ppermute | solution.py:18
  29.9 39.5 %collective-permute-start.15 = (bf16[1,2,128,1024]{2,3,1,0:T(8,128)(2,1)S(1)}, bf16[1,2,128,1024]{2,3,1,0:T(8,128)(2,1)}, u32[]{:S(2)}, u32[]{:S(2)}) collective-permute-start(bf16[1,2,128,1024]{2,3,1,0:T(8,128)(2,1)S(1)} %get-tuple-element.181), channel_id=1, source_target_pairs={{0,16},{4,20},{8,24},{12,28},{16,0},{20,4},{24,8},{28,12},{1,17},{... | collective-permute-start | bytes 1572872 | tf_op jit(solution)/shard_map/ppermute | solution.py:18
  46.5 28.1 %collective-permute-start.5 = (bf16[4,128,768]{2,1,0:T(8,128)(2,1)S(1)}, bf16[4,128,768]{2,1,0:T(8,128)(2,1)S(1)}, u32[]{:S(2)}, u32[]{:S(2)}) collective-permute-start(bf16[4,128,768]{2,1,0:T(8,128)(2,1)S(1)} %bitcast.567), channel_id=1, source_target_pairs={{0,4},{4,0},{8,12},{12,8},{16,20},{20,16},{24,28},{28,24},{1,5},{5... | collective-permute-start | bytes 2359304 | tf_op jit(solution)/shard_map/ppermute | solution.py:18
  50.4 24.7 %collective-permute-start.21 = (bf16[256,1024]{1,0:T(8,128)(2,1)}, bf16[256,1024]{1,0:T(8,128)(2,1)}, u32[]{:S(2)}, u32[]{:S(2)}) collective-permute-start(bf16[256,1024]{1,0:T(8,128)(2,1)} %get-tuple-element.149), channel_id=1, source_target_pairs={{0,2},{1,3},{2,0},{3,1},{4,6},{5,7},{6,4},{7,5},{8,10},{9,11},{10,... | collective-permute-start | bytes 1572872 | tf_op jit(solution)/shard_map/ppermute | solution.py:18
  74.6 131.0 %collective-permute-start.42 = (bf16[256,1024]{1,0:T(8,128)(2,1)}, bf16[256,1024]{1,0:T(8,128)(2,1)}, u32[]{:S(2)}, u32[]{:S(2)}) collective-permute-start(bf16[256,1024]{1,0:T(8,128)(2,1)} %get-tuple-element.160), channel_id=1, source_target_pairs={{0,2},{1,3},{2,0},{3,1},{4,6},{5,7},{6,4},{7,5},{8,10},{9,11},{10,... | collective-permute-start | bytes 1572872 | tf_op jit(solution)/shard_map/ppermute | solution.py:18
  75.0 165.2 %collective-permute-start.41 = (bf16[256,1024]{1,0:T(8,128)(2,1)}, bf16[256,1024]{1,0:T(8,128)(2,1)}, u32[]{:S(2)}, u32[]{:S(2)}) collective-permute-start(bf16[256,1024]{1,0:T(8,128)(2,1)} %get-tuple-element.160), channel_id=1, source_target_pairs={{0,1},{1,0},{2,3},{3,2},{4,5},{5,4},{6,7},{7,6},{8,9},{9,8},{10,11... | collective-permute-start | bytes 1572872 | tf_op jit(solution)/shard_map/ppermute | solution.py:18
  89.7 35.0 %collective-permute-start.16 = (bf16[2,2,128,1024]{2,3,1,0:T(8,128)(2,1)}, bf16[2,2,128,1024]{2,3,1,0:T(8,128)(2,1)}, u32[]{:S(2)}, u32[]{:S(2)}) collective-permute-start(bf16[2,2,128,1024]{2,3,1,0:T(8,128)(2,1)} %maximum_select_fusion.5), channel_id=1, source_target_pairs={{0,8},{4,12},{8,0},{12,4},{16,24},{20,28},{24,16},{28,20},{1,9},{5... | collective-permute-start | bytes 3145736 | tf_op jit(solution)/shard_map/ppermute | solution.py:18
  91.5 38.4 %collective-permute-start.11 = (bf16[4,128,1024]{2,1,0:T(8,128)(2,1)}, bf16[4,128,1024]{2,1,0:T(8,128)(2,1)}, u32[]{:S(2)}, u32[]{:S(2)}) collective-permute-start(bf16[4,128,1024]{2,1,0:T(8,128)(2,1)} %bitcast.30), channel_id=1, source_target_pairs={{0,4},{4,0},{8,12},{12,8},{16,20},{20,16},{24,28},{28,24},{1,5},{5... | collective-permute-start | bytes 3145736 | tf_op jit(solution)/shard_map/ppermute | solution.py:18
  136.3 48.1 %collective-permute-start.17 = (bf16[4,2,128,1024]{2,3,1,0:T(8,128)(2,1)}, bf16[4,2,128,1024]{2,3,1,0:T(8,128)(2,1)}, u32[]{:S(2)}, u32[]{:S(2)}) collective-permute-start(bf16[4,2,128,1024]{2,3,1,0:T(8,128)(2,1)} %bitcast.46), channel_id=1, source_target_pairs={{0,4},{4,0},{8,12},{12,8},{16,20},{20,16},{24,28},{28,24},{1,5},{5... | collective-permute-start | bytes 6291464 | tf_op jit(solution)/shard_map/ppermute | solution.py:18
  148.4 50.8 %collective-permute-start.26 = (bf16[256,1024]{1,0:T(8,128)(2,1)}, bf16[256,1024]{1,0:T(8,128)(2,1)}, u32[]{:S(2)}, u32[]{:S(2)}) collective-permute-start(bf16[256,1024]{1,0:T(8,128)(2,1)} %get-tuple-element.198), channel_id=1, source_target_pairs={{0,1},{1,0},{2,3},{3,2},{4,5},{5,4},{6,7},{7,6},{8,9},{9,8},{10,11... | collective-permute-start | bytes 1572872 | tf_op jit(solution)/shard_map/ppermute | solution.py:18
  159.3 42.0 %collective-permute-start.13 = (bf16[256,1024]{1,0:T(8,128)(2,1)}, bf16[256,1024]{1,0:T(8,128)(2,1)}, u32[]{:S(2)}, u32[]{:S(2)}) collective-permute-start(bf16[256,1024]{1,0:T(8,128)(2,1)} %get-tuple-element.197), channel_id=1, source_target_pairs={{0,2},{1,3},{2,0},{3,1},{4,6},{5,7},{6,4},{7,5},{8,10},{9,11},{10,... | collective-permute-start | bytes 1572872 | tf_op jit(solution)/shard_map/ppermute | solution.py:18
  213.8 26.4 %collective-permute-start.43 = (bf16[256,1024]{1,0:T(8,128)(2,1)}, bf16[256,1024]{1,0:T(8,128)(2,1)S(1)}, u32[]{:S(2)}, u32[]{:S(2)}) collective-permute-start(bf16[256,1024]{1,0:T(8,128)(2,1)} %collective-permute-done.42), channel_id=1, source_target_pairs={{0,1},{1,0},{2,3},{3,2},{4,5},{5,4},{6,7},{7,6},{8,9},{9,8},{10,11... | collective-permute-start | bytes 1572872 | tf_op jit(solution)/shard_map/ppermute | solution.py:18
  232.7 39.7 %collective-permute-start.34 = (bf16[2,256,1024]{2,1,0:T(8,128)(2,1)}, bf16[2,256,1024]{2,1,0:T(8,128)(2,1)}, u32[]{:S(2)}, u32[]{:S(2)}) collective-permute-start(bf16[2,256,1024]{2,1,0:T(8,128)(2,1)} %fusion.63), channel_id=1, source_target_pairs={{0,1},{1,0},{2,3},{3,2},{4,5},{5,4},{6,7},{7,6},{8,9},{9,8},{10,11... | collective-permute-start | bytes 3145736 | tf_op jit(solution)/shard_map/ppermute | solution.py:18
  236.2 39.7 %collective-permute-start.18 = (bf16[2,256,1024]{2,1,0:T(8,128)(2,1)}, bf16[2,256,1024]{2,1,0:T(8,128)(2,1)S(1)}, u32[]{:S(2)}, u32[]{:S(2)}) collective-permute-start(bf16[2,256,1024]{2,1,0:T(8,128)(2,1)} %fusion.61), channel_id=1, source_target_pairs={{0,1},{1,0},{2,3},{3,2},{4,5},{5,4},{6,7},{7,6},{8,9},{9,8},{10,11... | collective-permute-start | bytes 3145736 | tf_op jit(solution)/shard_map/ppermute | solution.py:18
  240.1 36.5 %collective-permute-start.29 = (bf16[2,256,1024]{2,1,0:T(8,128)(2,1)}, bf16[2,256,1024]{2,1,0:T(8,128)(2,1)S(1)}, u32[]{:S(2)}, u32[]{:S(2)}) collective-permute-start(bf16[2,256,1024]{2,1,0:T(8,128)(2,1)} %fusion.62), channel_id=1, source_target_pairs={{0,1},{1,0},{2,3},{3,2},{4,5},{5,4},{6,7},{7,6},{8,9},{9,8},{10,11... | collective-permute-start | bytes 3145736 | tf_op jit(solution)/shard_map/ppermute | solution.py:18
  250.0 29.1 %collective-permute-start.44 = (bf16[2,256,1024]{2,1,0:T(8,128)(2,1)S(1)}, bf16[2,256,1024]{2,1,0:T(8,128)(2,1)S(1)}, u32[]{:S(2)}, u32[]{:S(2)}) collective-permute-start(bf16[2,256,1024]{2,1,0:T(8,128)(2,1)S(1)} %fusion.65), channel_id=1, source_target_pairs={{0,1},{1,0},{2,3},{3,2},{4,5},{5,4},{6,7},{7,6},{8,9},{9,8},{10,11... | collective-permute-start | bytes 3145736 | tf_op jit(solution)/shard_map/ppermute | solution.py:18
  276.3 23.8 %collective-permute-start.19 = (bf16[1,256,1024]{2,1,0:T(8,128)(2,1)S(1)}, bf16[1,256,1024]{2,1,0:T(8,128)(2,1)S(1)}, u32[]{:S(2)}, u32[]{:S(2)}) collective-permute-start(bf16[1,256,1024]{2,1,0:T(8,128)(2,1)S(1)} %fusion.89), channel_id=1, source_target_pairs={{0,2},{1,3},{2,0},{3,1},{4,6},{5,7},{6,4},{7,5},{8,10},{9,11},{10,... | collective-permute-start | bytes 1572872 | tf_op jit(solution)/shard_map/ppermute | solution.py:18
  277.2 34.1 %collective-permute-start.30 = (bf16[1,256,1024]{2,1,0:T(8,128)(2,1)S(1)}, bf16[1,256,1024]{2,1,0:T(8,128)(2,1)S(1)}, u32[]{:S(2)}, u32[]{:S(2)}) collective-permute-start(bf16[1,256,1024]{2,1,0:T(8,128)(2,1)S(1)} %fusion.91), channel_id=1, source_target_pairs={{0,2},{1,3},{2,0},{3,1},{4,6},{5,7},{6,4},{7,5},{8,10},{9,11},{10,... | collective-permute-start | bytes 1572872 | tf_op jit(solution)/shard_map/ppermute | solution.py:18
  279.5 42.3 %collective-permute-start.45 = (bf16[1,256,1024]{2,1,0:T(8,128)(2,1)S(1)}, bf16[1,256,1024]{2,1,0:T(8,128)(2,1)S(1)}, u32[]{:S(2)}, u32[]{:S(2)}) collective-permute-start(bf16[1,256,1024]{2,1,0:T(8,128)(2,1)S(1)} %fusion.94), channel_id=1, source_target_pairs={{0,2},{1,3},{2,0},{3,1},{4,6},{5,7},{6,4},{7,5},{8,10},{9,11},{10,... | collective-permute-start | bytes 1572872 | tf_op jit(solution)/shard_map/ppermute | solution.py:18
  283.0 104.5 %collective-permute-start.69 = (bf16[4,2,128,1024]{3,2,1,0:T(8,128)(2,1)}, bf16[4,2,128,1024]{3,2,1,0:T(8,128)(2,1)}, u32[]{:S(2)}, u32[]{:S(2)}) collective-permute-start(bf16[4,2,128,1024]{3,2,1,0:T(8,128)(2,1)} %bitcast.540), channel_id=1, source_target_pairs={{0,4},{4,0},{8,12},{12,8},{16,20},{20,16},{24,28},{28,24},{1,5},{5... | collective-permute-start | bytes 6291464 | tf_op jit(solution)/shard_map/ppermute | solution.py:18
  356.4 44.3 %collective-permute-start.59 = (bf16[4,128,1024]{2,1,0:T(8,128)(2,1)}, bf16[4,128,1024]{2,1,0:T(8,128)(2,1)}, u32[]{:S(2)}, u32[]{:S(2)}) collective-permute-start(bf16[4,128,1024]{2,1,0:T(8,128)(2,1)} %dynamic-slice_bitcast_fusion), channel_id=1, source_target_pairs={{0,4},{4,0},{8,12},{12,8},{16,20},{20,16},{24,28},{28,24},{1,5},{5... | collective-permute-start | bytes 3145736 | tf_op jit(solution)/shard_map/ppermute | solution.py:18
  358.1 28.0 %collective-permute-start.68 = (f32[64,128]{1,0:T(8,128)S(1)}, f32[64,128]{1,0:T(8,128)S(1)}, u32[]{:S(2)}, u32[]{:S(2)}) collective-permute-start(f32[64,128]{1,0:T(8,128)S(1)} %add.490), channel_id=1, source_target_pairs={{0,16},{4,20},{8,24},{12,28},{16,0},{20,4},{24,8},{28,12},{1,17},{... | collective-permute-start | bytes 98312 | tf_op jit(solution)/shard_map/ppermute | solution.py:18
  379.9 24.9 %collective-permute-start.39 = (bf16[2,256,1024]{2,1,0:T(8,128)(2,1)}, bf16[2,256,1024]{2,1,0:T(8,128)(2,1)}, u32[]{:S(2)}, u32[]{:S(2)}) collective-permute-start(bf16[2,256,1024]{2,1,0:T(8,128)(2,1)} %fusion.64), channel_id=1, source_target_pairs={{0,1},{1,0},{2,3},{3,2},{4,5},{5,4},{6,7},{7,6},{8,9},{9,8},{10,11... | collective-permute-start | bytes 3145736 | tf_op jit(solution)/shard_map/ppermute | solution.py:18
  386.1 23.0 %collective-permute-start.49 = (bf16[2,256,1024]{2,1,0:T(8,128)(2,1)}, bf16[2,256,1024]{2,1,0:T(8,128)(2,1)S(1)}, u32[]{:S(2)}, u32[]{:S(2)}) collective-permute-start(bf16[2,256,1024]{2,1,0:T(8,128)(2,1)} %fusion.66), channel_id=1, source_target_pairs={{0,1},{1,0},{2,3},{3,2},{4,5},{5,4},{6,7},{7,6},{8,9},{9,8},{10,11... | collective-permute-start | bytes 3145736 | tf_op jit(solution)/shard_map/ppermute | solution.py:18
  391.1 51.4 %collective-permute-start.70 = (bf16[2,2,128,1024]{3,2,1,0:T(8,128)(2,1)}, bf16[2,2,128,1024]{3,2,1,0:T(8,128)(2,1)}, u32[]{:S(2)}, u32[]{:S(2)}) collective-permute-start(bf16[2,2,128,1024]{3,2,1,0:T(8,128)(2,1)} %fusion.60), channel_id=1, source_target_pairs={{0,8},{4,12},{8,0},{12,4},{16,24},{20,28},{24,16},{28,20},{1,9},{5... | collective-permute-start | bytes 3145736 | tf_op jit(solution)/shard_map/ppermute | solution.py:18
  400.0 25.7 %collective-permute-start.57 = (bf16[2,128,768]{2,1,0:T(8,128)(2,1)S(1)}, bf16[2,128,768]{2,1,0:T(8,128)(2,1)S(1)}, u32[]{:S(2)}, u32[]{:S(2)}) collective-permute-start(bf16[2,128,768]{2,1,0:T(8,128)(2,1)S(1)} %fusion.96), channel_id=1, source_target_pairs={{0,8},{4,12},{8,0},{12,4},{16,24},{20,28},{24,16},{28,20},{1,9},{5... | collective-permute-start | bytes 1179656 | tf_op jit(solution)/shard_map/ppermute | solution.py:18
  403.7 45.6 %collective-permute-start.60 = (bf16[2,128,1024]{2,1,0:T(8,128)(2,1)}, bf16[2,128,1024]{2,1,0:T(8,128)(2,1)}, u32[]{:S(2)}, u32[]{:S(2)}) collective-permute-start(bf16[2,128,1024]{2,1,0:T(8,128)(2,1)} %fusion.87), channel_id=1, source_target_pairs={{0,8},{4,12},{8,0},{12,4},{16,24},{20,28},{24,16},{28,20},{1,9},{5... | collective-permute-start | bytes 1572872 | tf_op jit(solution)/shard_map/ppermute | solution.py:18
  407.4 44.2 %collective-permute-start.40 = (bf16[1,256,1024]{2,1,0:T(8,128)(2,1)}, bf16[1,256,1024]{2,1,0:T(8,128)(2,1)S(1)}, u32[]{:S(2)}, u32[]{:S(2)}) collective-permute-start(bf16[1,256,1024]{2,1,0:T(8,128)(2,1)} %fusion.93), channel_id=1, source_target_pairs={{0,2},{1,3},{2,0},{3,1},{4,6},{5,7},{6,4},{7,5},{8,10},{9,11},{10,... | collective-permute-start | bytes 1572872 | tf_op jit(solution)/shard_map/ppermute | solution.py:18
  428.2 23.4 %collective-permute-start.50 = (bf16[1,256,1024]{2,1,0:T(8,128)(2,1)}, bf16[1,256,1024]{2,1,0:T(8,128)(2,1)S(1)}, u32[]{:S(2)}, u32[]{:S(2)}) collective-permute-start(bf16[1,256,1024]{2,1,0:T(8,128)(2,1)} %fusion.95), channel_id=1, source_target_pairs={{0,2},{1,3},{2,0},{3,1},{4,6},{5,7},{6,4},{7,5},{8,10},{9,11},{10,... | collective-permute-start | bytes 1572872 | tf_op jit(solution)/shard_map/ppermute | solution.py:18
  445.9 42.4 %collective-permute-start.71 = (bf16[1,2,128,1024]{3,2,1,0:T(8,128)(2,1)}, bf16[1,2,128,1024]{3,2,1,0:T(8,128)(2,1)}, u32[]{:S(2)}, u32[]{:S(2)}) collective-permute-start(bf16[1,2,128,1024]{3,2,1,0:T(8,128)(2,1)} %dynamic-slice_convert_fusion.1), channel_id=1, source_target_pairs={{0,16},{4,20},{8,24},{12,28},{16,0},{20,4},{24,8},{28,12},{1,17},{... | collective-permute-start | bytes 1572872 | tf_op jit(solution)/shard_map/ppermute | solution.py:18
  450.5 34.0 %collective-permute-start.61 = (bf16[1,128,1024]{2,1,0:T(8,128)(2,1)S(1)}, bf16[1,128,1024]{2,1,0:T(8,128)(2,1)S(1)}, u32[]{:S(2)}, u32[]{:S(2)}) collective-permute-start(bf16[1,128,1024]{2,1,0:T(8,128)(2,1)S(1)} %dynamic-slice_convert_fusion.4), channel_id=1, source_target_pairs={{0,16},{4,20},{8,24},{12,28},{16,0},{20,4},{24,8},{28,12},{1,17},{... | collective-permute-start | bytes 786440 | tf_op jit(solution)/shard_map/ppermute | solution.py:18
  (144 other events, 1215.1 us)
